TPU v7x, 32 devices: a whole 2x2x4 slice. The times are simulated.
32 devices in a mesh: groups: 2 (over y), dp: 4 (over z), rep: 4 (over x, core).
Axes of the slice: x: 2, y: 2, z: 4, core: 2. Of those that a mesh axis runs over, the one named last changes fastest.
Arguments:
- latent_store: bfloat16 [8, 48, 576, 128], P(('groups', 'dp'), 'rep'), parts along dimension 0, may hold values from -6 to 6
- page_rank: int32 [8, 48], P('groups', 'rep'), parts along dimension 0, may hold values from 0 to 3, as said below
- page_index: int32 [8, 48], P('groups', 'rep'), parts along dimension 0, may hold values from 0 to 11, as said below
- lengths: int32 [8, 1], P('groups'), parts along dimension 0, may hold values from 1536 to 6144, as said below
- queries: bfloat16 [16, 36864], P(('groups', 'dp')), parts along dimension 0, may hold values from -250 to 250
- new_latent: bfloat16 [16, 576], P(('groups', 'dp')), parts along dimension 0, may hold values from -4 to 4
- up_value: bfloat16 [64, 512, 128], P('dp'), may hold values from -0.25 to 0.25
- out_proj: bfloat16 [8192, 7168], P('dp', 'rep'), may hold values from -0.0625 to 0.0625
- residual: bfloat16 [16, 7168], P(('groups', 'dp'), 'rep'), parts along dimension 0, may hold values from -11 to 11
- norm_gain: float32 [7168], P('rep'), may hold values from 0.1 to 1.9
- w_gate: bfloat16 [7168, 12288], P('rep', 'dp'), may hold values from -0.0625 to 0.0625
- w_up: bfloat16 [7168, 12288], P('rep', 'dp'), may hold values from -0.0625 to 0.0625
- w_down: bfloat16 [12288, 7168], P('dp', 'rep'), may hold values from -0.0546875 to 0.0546875
Outputs:
- layer_out: bfloat16 [16, 7168], P(('groups', 'dp'), 'rep'), parts along dimension 0
There are 2 independent parts, one for each index of `groups`. A program takes and returns all parts, laid end to end along the dimension named above; an argument that names none is the same for every part. Nothing has to cross between parts.
Inputs may be any that keep to these rules, and one draw needn't show every extreme that they name: page_rank[d, q] is the storage rank holding slot q of rank d, on its device with rep index q // 12; one storage device holds at most 3 slot of one rank, and some holds exactly 3. page_index[d, q] is the slot's page among the 12 pages of its storage device; over all ranks every page of every storage device is named by exactly one slot. `lengths`: some request has exactly 6144 tokens.
All inputs are finite; a program needn't handle non-finite values.
Results may differ from a plain program's by a relative error of at most 0.015.
Values may be sent and summed in bfloat16 or wider, within the bound.
No kernel may reach another device: no remote copies, remote signals or barrier semaphores. Data moves between devices by JAX's collectives and lax.ppermute only.
A program may use at most 128 MiB of HBM per device.

v0:
```python
import math

import jax
import jax.numpy as jnp
from jax import lax
from jax.sharding import PartitionSpec as P

D = 7168
CKV = 512
PAGE = 128
PAGES = 48


score_scale = 1.0 / math.sqrt(192.0)
epsilon = 1e-06
mask_value = -1e30


def merged_2(array, axis, join):
    gathered = jax.tree.map(
        lambda a, kind: lax.all_gather(a.astype(kind), axis),
        array,
        jax.tree.map(lambda a: jnp.bfloat16 if a.dtype == jnp.float32 else a.dtype, array),
    )

    def take(source):
        return jax.tree.map(
            lambda a, own: lax.dynamic_index_in_dim(a, source, 0, False).astype(own.dtype),
            gathered,
            array,
        )

    return lax.fori_loop(
        1, lax.axis_size(axis), lambda source, state: join(state, take(source)), take(0)
    )


def page_partials(page_keys, page_queries, key_counts):
    scores = (
        jnp.einsum("pshl,plt->psht", page_queries, page_keys, preferred_element_type=jnp.float32)
        * score_scale
    )
    places = lax.broadcasted_iota(jnp.int32, scores.shape, 3)
    visible = places < key_counts[:, None, None, None]
    scores = jnp.where(visible, scores, mask_value)
    row_peak = jnp.max(scores, axis=3)
    weights = jnp.where(visible, jnp.exp(scores - row_peak[..., None]), 0.0)
    row_total = jnp.sum(weights, axis=3)
    partial_value = jnp.einsum(
        "psht,pct->pshc",
        weights.astype(jnp.bfloat16),
        page_keys[:, :CKV, :],
        preferred_element_type=jnp.float32,
    )
    return (partial_value, row_peak, row_total)


def join_pages(partial_value, row_peak, row_total, slot_request, requests):
    owner_mask = slot_request[None, :] == jnp.arange(requests, dtype=jnp.int32)[:, None]
    spread = owner_mask[:, :, None, None]
    best_peak = jnp.max(jnp.where(spread, row_peak[None], mask_value), axis=1)
    factor = jnp.where(spread, jnp.exp(row_peak[None] - best_peak[:, None]), 0.0)
    joined = jnp.einsum("jpsh,pshc->jshc", factor, partial_value, precision=lax.Precision.HIGHEST)
    summed = jnp.sum(factor * row_total[None], axis=1)
    return (joined, best_peak, summed)


def combine(former, latter):
    former_sum, former_peak, former_total = former
    latter_sum, latter_peak, latter_total = latter
    highest = jnp.maximum(former_peak, latter_peak)
    former_scale = jnp.exp(former_peak - highest)
    latter_scale = jnp.exp(latter_peak - highest)
    merged_sum = former_sum * former_scale[..., None] + latter_sum * latter_scale[..., None]
    return (merged_sum, highest, former_total * former_scale + latter_total * latter_scale)


def fresh_partial(query_rows, fresh_rows, active):
    scores = (
        jnp.einsum("jshl,jul->jshu", query_rows, fresh_rows, preferred_element_type=jnp.float32)
        * score_scale
    )
    step_query = lax.broadcasted_iota(jnp.int32, scores.shape, 1)
    step_key = lax.broadcasted_iota(jnp.int32, scores.shape, 3)
    visible = (step_key <= step_query) & active
    scores = jnp.where(visible, scores, mask_value)
    row_peak = jnp.max(scores, axis=3)
    weights = jnp.where(visible, jnp.exp(scores - row_peak[..., None]), 0.0)
    row_total = jnp.sum(weights, axis=3)
    partial_value = jnp.einsum(
        "jshu,juc->jshc",
        weights.astype(jnp.bfloat16),
        fresh_rows[:, :, :CKV],
        preferred_element_type=jnp.float32,
    )
    return (partial_value, row_peak, row_total)


def on_device(
    latent_store,
    page_rank,
    page_index,
    lengths,
    queries,
    new_latent,
    up_value,
    out_proj,
    residual,
    norm_gain,
    w_gate,
    w_up,
    w_down,
):
    my_rank = lax.axis_index("dp")
    my_column = lax.axis_index("rep")
    rank_count, slot_count = page_rank.shape
    capacity = (slot_count + rank_count - 1) // rank_count
    requests = lengths.shape[1]
    rows_here = residual.shape[0]
    steps_count = rows_here // requests
    latent_width = new_latent.shape[1]
    head_count = queries.shape[1] // latent_width
    query_rows = queries.reshape(requests, steps_count, head_count, latent_width)
    fresh_rows = new_latent.reshape(requests, steps_count, latent_width)
    slot_order = jnp.arange(slot_count, dtype=jnp.int32)
    request_ids = jnp.arange(requests, dtype=jnp.int32)
    cap_ids = jnp.arange(capacity, dtype=jnp.int32)
    global_slot = my_column * slot_count + slot_order
    slot_request = global_slot // PAGES
    slot_page = global_slot % PAGES
    own_lengths = lax.dynamic_index_in_dim(lengths, my_rank, 0, keepdims=False)
    slot_length = jnp.sum(
        jnp.where(slot_request[:, None] == request_ids[None, :], own_lengths[None, :], 0), axis=1
    )
    key_counts = jnp.clip(slot_length - slot_page * PAGE, 0, PAGE)
    my_sources = lax.dynamic_index_in_dim(page_rank, my_rank, 0, keepdims=False)
    earlier = (my_sources[None, :] == my_sources[:, None]) & (
        slot_order[None, :] < slot_order[:, None]
    )
    arrival_rank = jnp.sum(earlier.astype(jnp.int32), axis=1)
    arrival_slot = my_sources * capacity + arrival_rank
    held_here = page_rank == my_rank
    held_order = jnp.cumsum(held_here.astype(jnp.int32), axis=1) - 1
    selector = held_here[:, None, :] & (held_order[:, None, :] == cap_ids[None, :, None])
    sent_valid = jnp.any(selector, axis=2).reshape(-1)
    sent_page = jnp.sum(jnp.where(selector, page_index[:, None, :], 0), axis=2).reshape(-1)
    stored = latent_store[0]
    outgoing = jnp.take(stored, sent_page, axis=0)
    outgoing = jnp.where(sent_valid[:, None, None], outgoing, jnp.zeros_like(outgoing))
    arrived = lax.all_to_all(outgoing, "dp", split_axis=0, concat_axis=0, tiled=True)
    restored = jnp.take(arrived, arrival_slot, axis=0)
    page_queries = jnp.take(query_rows, slot_request, axis=0)
    partial_value, row_peak, row_total = page_partials(restored, page_queries, key_counts)
    joined = join_pages(partial_value, row_peak, row_total, slot_request, requests)
    local_part = combine(joined, fresh_partial(query_rows, fresh_rows, my_column == 0))
    merged = merged_2(local_part, "rep", combine)
    attention = (
        (merged[0] / merged[2][..., None]).astype(jnp.bfloat16).reshape(rows_here, head_count, CKV)
    )
    headed = lax.all_to_all(attention, "dp", split_axis=1, concat_axis=0, tiled=True)
    values = jnp.einsum("rhc,hcv->rhv", headed, up_value, preferred_element_type=jnp.float32)
    values = values.astype(jnp.bfloat16).reshape(headed.shape[0], -1)
    picked = values
    attn_out = lax.psum_scatter(
        jnp.dot(picked, out_proj, preferred_element_type=jnp.float32).astype(jnp.bfloat16),
        "dp",
        scatter_dimension=0,
        tiled=True,
    ).astype(jnp.float32)
    mixed_rows = residual.astype(jnp.float32) + attn_out
    squares = lax.psum(jnp.sum(mixed_rows * mixed_rows, axis=1), "rep")
    normed = (mixed_rows * lax.rsqrt(squares / D + epsilon)[:, None] * norm_gain).astype(
        jnp.bfloat16
    )
    piece = lax.all_gather(normed, "dp", axis=0, tiled=True)
    gate_part = jnp.dot(piece, w_gate, preferred_element_type=jnp.float32)
    up_part = jnp.dot(piece, w_up, preferred_element_type=jnp.float32)
    partial_rows = jnp.concatenate([gate_part, up_part], axis=1)
    gate_up = lax.psum(partial_rows.astype(jnp.bfloat16), "rep").astype(jnp.float32)
    hidden_width = w_gate.shape[1]
    hidden = (jax.nn.silu(gate_up[:, :hidden_width]) * gate_up[:, hidden_width:]).astype(
        jnp.bfloat16
    )
    picked = hidden
    mlp_out = lax.psum_scatter(
        jnp.dot(picked, w_down, preferred_element_type=jnp.float32).astype(jnp.bfloat16),
        "dp",
        scatter_dimension=0,
        tiled=True,
    ).astype(jnp.float32)
    return (mixed_rows + mlp_out).astype(jnp.bfloat16)


def solution(mesh):
    in_specs = (
        P(("groups", "dp"), "rep", None, None),
        P("groups", "rep"),
        P("groups", "rep"),
        P("groups", None),
        P(("groups", "dp"), None),
        P(("groups", "dp"), None),
        P("dp", None, None),
        P("dp", "rep"),
        P(("groups", "dp"), "rep"),
        P("rep"),
        P("rep", "dp"),
        P("rep", "dp"),
        P("dp", "rep"),
    )
    out_specs = P(("groups", "dp"), "rep")
    return jax.shard_map(
        on_device, mesh=mesh, in_specs=in_specs, out_specs=out_specs, check_vma=False
    )
```

profile of v0, /device:TPU:0, one launch (start us, length us, event | category | flops | bytes accessed | tf_op | source)
XLA Modules:
  0.0 225.6 jit_solution(1305932446610789168)
XLA Ops:
  6.5 0.0 copy-start
  6.5 0.8 fusion.66
  7.4 0.2 reduce_window_sum.11
  7.6 0.1 fusion.45
  7.7 0.8 select_reduce_fusion.1
  8.5 0.1 copy.21
  8.6 0.1 reshape.396
  8.8 0.1 copy.20
  8.9 0.1 broadcast_in_dim.122
  9.0 3.5 %gather_fusion = bf16[12,576,128]{2,1,0:T(8,128)(2,1)} fusion(bf16[12,576,128]{2,1,0:T(8,128)(2,1)} %bitcast.145, s32[1024]{0:T(1024)S(1)} %pad_clamp_fusion.1), kind=kCustom, calls=%fused_computation.clone | custom fusion | bytes 3538992 | tf_op jit(solution)/shard_map/jit(_take)/gather | solution.py:148
  12.5 2.9 %select_select_fusion = bf16[12,576,128]{2,1,0:T(8,128)(2,1)} fusion(bf16[12,576,128]{2,1,0:T(8,128)(2,1)} %gather_fusion, pred[12]{0:T(512)(128)(4,1)S(1)} %get-tuple-element.237, pred[12]{0:T(512)(128)(4,1)S(1)} %broadcast_in_dim.122), kind=kLoop, calls=%fused_computation.26 | loop fusion | flops 1769472 | bytes 3538968 | tf_op jit(solution)/shard_map/jit(_where)/select_n | solution.py:149
  15.4 6.5 %all-to-all-start = ((bf16[12,576,128]{2,1,0:T(8,128)(2,1)}), bf16[12,576,128]{2,1,0:T(8,128)(2,1)}, u32[]{:S(2)}, u32[]{:S(2)}) async-start(bf16[12,576,128]{2,1,0:T(8,128)(2,1)} %select_select_fusion), calls=%async_computation | async-start | bytes 3538944 | tf_op jit(solution)/shard_map/all_to_all | solution.py:150
  21.9 0.0 copy-done.1
  21.9 0.2 reshape.402
  22.1 0.0 copy-done.6
  22.1 0.6 constant_dynamic-slice_fusion.3
  22.7 0.6 fusion.60
  23.3 0.2 convert_reduce_fusion
  23.5 0.0 copy-done.3
  23.5 0.2 fusion.68
  23.8 39.4 %all-to-all-done = bf16[12,576,128]{2,1,0:T(8,128)(2,1)} async-done(((bf16[12,576,128]{2,1,0:T(8,128)(2,1)}), bf16[12,576,128]{2,1,0:T(8,128)(2,1)}, u32[]{:S(2)}, u32[]{:S(2)}) %all-to-all-start) | async-done | bytes 1769504 | tf_op jit(solution)/shard_map/all_to_all | solution.py:150
  63.2 3.5 %gather_fusion.1 = bf16[12,576,128]{2,1,0:T(8,128)(2,1)} fusion(bf16[12,576,128]{2,1,0:T(8,128)(2,1)} %all-to-all-done, s32[1024]{0:T(1024)S(1)} %pad_clamp_fusion), kind=kCustom, calls=%fused_computation.1.clone | custom fusion | bytes 3538992 | tf_op jit(solution)/shard_map/jit(_take)/gather | solution.py:151
  66.7 1.7 broadcast_select_fusion
  68.4 0.8 fusion.67
  69.3 0.6 fusion.30
  69.8 2.3 %fusion.13 = f32[12,2,64,512]{3,2,1,0:T(8,128)} fusion(bf16[12,576,128]{2,1,0:T(8,128)(2,1)S(1)} %broadcast_select_fusion, f32[12,2,64,128]{3,2,1,0:T(8,128)S(1)} %get-tuple-element.233, f32[12,2,64]{2,1,0:T(2,128)S(1)} %get-tuple-element.232, s32[12]{0:T(128)S(1)} %fusion.60), kind=kOutput, calls=%fused_computation.29 | convolution fusion | flops 202113024 | bytes 5517824 | tf_op jit(solution)/shard_map/psht,pct->pshc/dot_general | solution.py:49
  72.1 0.1 select_reduce_fusion
  72.3 0.1 multiply_reduce_fusion.1
  72.4 5.1 %all_gather.20 = bf16[4,1,2,64]{3,2,1,0:T(2,128)(2,1)S(1)} all-gather(bf16[1,1,2,64]{3,2,1,0:T(2,128)(2,1)S(1)} %fusion.50), channel_id=1, replica_groups=mesh['groups'=2,'dp'=4,'rep'=4] {'rep'}, dimensions={0}, use_global_device_ids=true | all-gather | bytes 1280 | tf_op jit(solution)/shard_map/all_gather | solution.py:21
  77.4 0.1 copy.29
  77.5 7.4 %fusion.7 = f32[2,64,1,512]{3,2,1,0:T(1,128)S(1)} fusion(f32[12,2,64,1]{0,3,2,1:T(1,128)S(1)} %copy.29, f32[12,2,64,512]{3,2,1,0:T(8,128)} %fusion.13), kind=kOutput, calls=%fused_computation.16 | convolution fusion | flops 9437184 | bytes 3414016 | tf_op jit(solution)/shard_map/jpsh,pshc->jshc/dot_general | solution.py:63
  84.9 0.2 fusion.25
  85.2 7.3 %all-gather = bf16[8,64,512]{2,1,0:T(8,128)(2,1)S(1)} all-gather(bf16[2,64,512]{2,1,0:T(8,128)(2,1)S(1)} %fusion.25), channel_id=2, replica_groups=mesh['groups'=2,'dp'=4,'rep'=4] {'rep'}, dimensions={0}, use_global_device_ids=true | all-gather | bytes 655360 | tf_op jit(solution)/shard_map/all_gather | solution.py:21
  92.5 5.1 %all_gather.19 = bf16[4,1,2,64]{3,2,1,0:T(2,128)(2,1)S(1)} all-gather(bf16[1,1,2,64]{3,2,1,0:T(2,128)(2,1)S(1)} %fusion.54), channel_id=1, replica_groups=mesh['groups'=2,'dp'=4,'rep'=4] {'rep'}, dimensions={0}, use_global_device_ids=true | all-gather | bytes 1280 | tf_op jit(solution)/shard_map/all_gather | solution.py:21
  97.5 0.6 while.19
  97.6 0.1 fusion.84
  97.8 0.1 fusion.84
  98.0 0.1 fusion.84
  98.1 0.1 copy.23
  98.2 1.0 fusion.38
  99.2 3.3 %all-to-all-start.1 = ((bf16[2,64,512]{2,0,1:T(2,128)(2,1)}), bf16[2,64,512]{2,0,1:T(2,128)(2,1)S(1)}, u32[]{:S(2)}, u32[]{:S(2)}) async-start(bf16[2,64,512]{2,0,1:T(2,128)(2,1)} %fusion.38), calls=%async_computation.1 | async-start | bytes 262144 | tf_op jit(solution)/shard_map/all_to_all | solution.py:160
  102.5 0.0 all-reduce.4.cloned.1.call-start
  102.6 0.6 dynamic-slice
  103.8 5.2 %all-to-all-done.1 = bf16[2,64,512]{2,0,1:T(2,128)(2,1)S(1)} async-done(((bf16[2,64,512]{2,0,1:T(2,128)(2,1)}), bf16[2,64,512]{2,0,1:T(2,128)(2,1)S(1)}, u32[]{:S(2)}, u32[]{:S(2)}) %all-to-all-start.1) | async-done | bytes 131104 | tf_op jit(solution)/shard_map/all_to_all | solution.py:160
  109.0 0.1 copy.40
  109.1 0.1 all_to_all.20
  109.2 0.0 copy-start.2
  109.2 0.0 copy-start.4
  109.2 4.4 %convolution_convert_fusion.3 = bf16[8,1792]{1,0:T(8,128)(2,1)S(1)} fusion(bf16[2048,1792]{1,0:T(8,128)(2,1)} %param.24, bf16[8,16,512]{2,0,1:T(8,128)(2,1)S(1)} %all_to_all.20, bf16[16,512,128]{2,1,0:T(8,128)(2,1)S(1)} %copy-done), kind=kOutput, calls=%fused_computation.21 | convolution fusion | flops 75528192 | bytes 9596928 | tf_op jit(solution)/shard_map/dot_general | solution.py:165
  113.6 17.5 %all-reduce = bf16[8,1792]{1,0:T(8,128)(2,1)S(1)} all-reduce(bf16[8,1792]{1,0:T(8,128)(2,1)S(1)} %convolution_convert_fusion.3), channel_id=3, replica_groups=mesh['groups'=2,'dp'=4,'rep'=4] {'dp'}, use_global_device_ids=true, to_apply=%region_12.14.clone | all-reduce | flops 14336 | bytes 57344
  131.1 0.1 multiply_reduce_fusion
  131.2 5.8 %psum.14 = f32[2]{0:T(128)S(1)} all-reduce(f32[2]{0:T(128)S(1)} %multiply_reduce_fusion), channel_id=1, replica_groups=mesh['groups'=2,'dp'=4,'rep'=4] {'rep'}, use_global_device_ids=true, to_apply=%region_14.16 | all-reduce | flops 2 | bytes 16 | tf_op jit(solution)/shard_map/psum | solution.py:171
  137.0 0.0 copy-done.4
  137.0 0.1 fusion.43
  137.1 13.2 %all-gather.1 = bf16[4,2,1792]{2,1,0:T(2,128)(2,1)S(1)} all-gather(bf16[1,2,1792]{2,1,0:T(2,128)(2,1)S(1)} %fusion.43), channel_id=1, replica_groups=mesh['groups'=2,'dp'=4,'rep'=4] {'dp'}, dimensions={0}, use_global_device_ids=true | all-gather | bytes 35840 | tf_op jit(solution)/shard_map/all_gather | solution.py:175
  150.3 5.7 %convolution_convert_fusion = bf16[8,3072]{1,0:T(8,128)(2,1)S(1)} fusion(bf16[8,1792]{1,0:T(8,128)(2,1)S(1)} %reshape.433, bf16[1792,3072]{1,0:T(8,128)(2,1)} %param.28), kind=kOutput, calls=%fused_computation.18 | convolution fusion | flops 88104960 | bytes 11087872 | tf_op jit(solution)/shard_map/dot_general | solution.py:177
  156.0 5.7 %convolution_convert_fusion.1 = bf16[8,3072]{1,0:T(8,128)(2,1)S(1)} fusion(bf16[8,1792]{1,0:T(8,128)(2,1)S(1)} %reshape.433, bf16[1792,3072]{1,0:T(8,128)(2,1)} %param.27), kind=kOutput, calls=%fused_computation.19 | convolution fusion | flops 88104960 | bytes 11087872 | tf_op jit(solution)/shard_map/dot_general | solution.py:176
  161.7 0.6 pad_maximum_fusion
  162.3 0.0 all-reduce.4.cloned.1.call-update
  162.3 30.3 %all-reduce.4.cloned.1.call-done = bf16[8,6144]{1,0:T(8,128)(2,1)} async-done(((bf16[8,6144]{1,0:T(8,128)(2,1)}), bf16[8,6144]{1,0:T(8,128)(2,1)}) %all-reduce.4.cloned.1.call-update) | async-done | bytes 98320 | tf_op jit(solution)/shard_map/psum | solution.py:179
  192.6 0.9 convert_element_type.203
  193.5 5.7 %convolution_convert_fusion.2 = bf16[8,1792]{1,0:T(8,128)(2,1)S(1)} fusion(bf16[3072,1792]{1,0:T(8,128)(2,1)} %param.29, f32[8,6144]{1,0:T(8,128)S(1)} %convert_element_type.203), kind=kOutput, calls=%fused_computation.20 | convolution fusion | flops 88242176 | bytes 11235328 | tf_op jit(solution)/shard_map/dot_general | solution.py:186
  199.2 19.0 %all-reduce.1 = bf16[8,1792]{1,0:T(8,128)(2,1)S(1)} all-reduce(bf16[8,1792]{1,0:T(8,128)(2,1)S(1)} %convolution_convert_fusion.2), channel_id=4, replica_groups=mesh['groups'=2,'dp'=4,'rep'=4] {'dp'}, use_global_device_ids=true, to_apply=%region_16.18.clone | all-reduce | flops 14336 | bytes 57344
  218.2 0.6 add_convert_fusion
  (34 shorter events, 0.3 us)
Async XLA Ops:
  6.5 102.6 %copy-start = (bf16[16,512,128]{2,1,0:T(8,128)(2,1)S(1)}, bf16[16,512,128]{2,1,0:T(8,128)(2,1)}, u32[]{:S(2)}) copy-start(bf16[16,512,128]{2,1,0:T(8,128)(2,1)} %param.23) | copy-start | bytes 6291460
  15.4 6.5 %copy-start.1 = (bf16[2,36864]{1,0:T(2,128)(2,1)S(1)}, bf16[2,36864]{1,0:T(2,128)(2,1)}, u32[]{:S(2)}) copy-start(bf16[2,36864]{1,0:T(2,128)(2,1)} %param.21) | copy-start | bytes 442372
  15.4 6.7 %copy-start.6 = (s32[4,1]{0,1:T(1,128)S(1)}, s32[4,1]{0,1:T(1,128)}, u32[]{:S(2)}) copy-start(s32[4,1]{0,1:T(1,128)} %param.20) | copy-start | bytes 52
  15.4 7.3 %copy-start.5 = (s32[4,12]{1,0:T(4,128)S(1)}, s32[4,12]{1,0:T(4,128)}, u32[]{:S(2)}) copy-start(s32[4,12]{1,0:T(4,128)} %param.18) | copy-start | bytes 580
  15.4 8.1 %copy-start.3 = (bf16[2,576]{1,0:T(2,128)(2,1)S(1)}, bf16[2,576]{1,0:T(2,128)(2,1)}, u32[]{:S(2)}) copy-start(bf16[2,576]{1,0:T(2,128)(2,1)} %param.22) | copy-start | bytes 6916
  15.4 47.8 %all-to-all-start = ((bf16[12,576,128]{2,1,0:T(8,128)(2,1)}), bf16[12,576,128]{2,1,0:T(8,128)(2,1)}, u32[]{:S(2)}, u32[]{:S(2)}) async-start(bf16[12,576,128]{2,1,0:T(8,128)(2,1)} %select_select_fusion), calls=%async_computation | async-start | bytes 3538944 | tf_op jit(solution)/shard_map/all_to_all | solution.py:150
  97.5 5.0 %copy-start.7 = (u32[32]{0:T(128)S(1)}, u32[32]{0:T(128)}, u32[]{:S(2)}) copy-start(u32[32]{0:T(128)} %constant.150) | copy-start | bytes 388
  99.2 9.8 %all-to-all-start.1 = ((bf16[2,64,512]{2,0,1:T(2,128)(2,1)}), bf16[2,64,512]{2,0,1:T(2,128)(2,1)S(1)}, u32[]{:S(2)}, u32[]{:S(2)}) async-start(bf16[2,64,512]{2,0,1:T(2,128)(2,1)} %fusion.38), calls=%async_computation.1 | async-start | bytes 262144 | tf_op jit(solution)/shard_map/all_to_all | solution.py:160
  102.5 90.1 %all-reduce.4.cloned.1.call-start = ((), (), s32[]{:S(2)}) async-start(), calls=%async_computation.2 | async-start | bytes 196608 | tf_op jit(solution)/shard_map/psum | solution.py:179
  109.2 21.9 %copy-start.2 = (bf16[2,1792]{1,0:T(2,128)(2,1)S(1)}, bf16[2,1792]{1,0:T(2,128)(2,1)}, u32[]{:S(2)}) copy-start(bf16[2,1792]{1,0:T(2,128)(2,1)} %param.25) | copy-start | bytes 21508
  109.2 27.9 %copy-start.4 = (f32[1792]{0:T(1024)S(1)}, f32[1792]{0:T(1024)}, u32[]{:S(2)}) copy-start(f32[1792]{0:T(1024)} %param.26) | copy-start | bytes 21508
Sparse Core Ops, SparseCore 0:
  162.4 30.1 all-reduce.3
where the time goes:
time: 226 us
  waiting for transfers between devices  74.9 us (33%)
  blocking collectives  72.8 us (32%)
  matrix products  32.4 us (14%)
  between operations  14.3 us (6%)
  other arithmetic  12.1 us (5%)
  starting transfers between devices  9.85 us (4%)
  local copies, waits for them, and re-layouts  9.15 us (4%)
    all_to_all x1, waiting for transfers between devices, on_device(): lax.all_to_all(outgoing, 'dp', split_axis=0, concat_axis=0, tiled=True)  39.4 us
    unnamed x2, blocking collectives  36.4 us
    psum x1, waiting for transfers between devices, on_device(): lax.psum(partial_rows.astype(jnp.bfloat16), 'rep').astype(jnp.float32)  30.3 us
    all_gather x3, blocking collectives, merged_2(): lax.all_gather(a.astype(kind), axis)  17.4 us
    all_gather x1, blocking collectives, on_device(): piece = lax.all_gather(normed, 'dp', axis=0, tiled=True)  13.2 us
    dot_general x1, matrix products, join_pages(): jnp.einsum('jpsh,pshc->jshc', factor, partial_value, precision=lax.Precis...  7.4 us
    all_to_all x1, starting transfers between devices, on_device(): lax.all_to_all(outgoing, 'dp', split_axis=0, concat_axis=0, tiled=True)  6.49 us
    psum x1, blocking collectives, on_device(): squares = lax.psum(jnp.sum(mixed_rows * mixed_rows, axis=1), 'rep')  5.84 us
  transfers between devices with their start and end apart: 3, of which 3 were waited for; matrix products, arithmetic and copies ran while one was open for 1% of the time, Pallas kernels for 0%

commit v1 on v0

--- a/solution.py
+++ b/solution.py
@@ -1,15 +1,18 @@
+import functools
 import math
 
 import jax
 import jax.numpy as jnp
 from jax import lax
+from jax.experimental import pallas as pl
+from jax.experimental.pallas import tpu as pltpu
 from jax.sharding import PartitionSpec as P
 
-D = 7168
 CKV = 512
 PAGE = 128
 PAGES = 48
-
+LANES = 128
+MIB = 1 << 20
 
 score_scale = 1.0 / math.sqrt(192.0)
 epsilon = 1e-06
@@ -96,7 +99,7 @@
     return (partial_value, row_peak, row_total)
 
 
-def on_device(
+def pages_moved(
     latent_store,
     page_rank,
     page_index,
@@ -169,7 +172,7 @@
     ).astype(jnp.float32)
     mixed_rows = residual.astype(jnp.float32) + attn_out
     squares = lax.psum(jnp.sum(mixed_rows * mixed_rows, axis=1), "rep")
-    normed = (mixed_rows * lax.rsqrt(squares / D + epsilon)[:, None] * norm_gain).astype(
+    normed = (mixed_rows * lax.rsqrt(squares / (norm_gain.shape[0] * lax.axis_size("rep")) + epsilon)[:, None] * norm_gain).astype(
         jnp.bfloat16
     )
     piece = lax.all_gather(normed, "dp", axis=0, tiled=True)
@@ -189,6 +192,366 @@
         tiled=True,
     ).astype(jnp.float32)
     return (mixed_rows + mlp_out).astype(jnp.bfloat16)
+
+
+def partners(array, axis):
+    size = lax.axis_size(axis)
+    return [
+        lax.ppermute(array, axis, [(i, i ^ step) for i in range(size)]) for step in range(1, size)
+    ]
+
+
+def thirds(value):
+    high = value.astype(jnp.bfloat16).astype(jnp.float32)
+    rest = value - high
+    middle = rest.astype(jnp.bfloat16).astype(jnp.float32)
+    return high, middle, (rest - middle).astype(jnp.bfloat16).astype(jnp.float32)
+
+
+def lane_ids(rows):
+    return lax.broadcasted_iota(jnp.int32, (rows, LANES), 1)
+
+
+def smem():
+    return pl.BlockSpec(memory_space=pltpu.SMEM)
+
+
+def vmem():
+    return pl.BlockSpec(memory_space=pltpu.VMEM)
+
+
+def locate_kernel(capacity, slots, place, lengths, rank_near, index_near, rank_far, index_far, page, count):
+    me, column = place[0], place[1]
+    ranks = lengths.shape[0]
+    for step in range(ranks):
+        rank = me ^ step
+        length = lengths[rank, 0]
+        for side, (table, index) in enumerate(((rank_near, index_near), (rank_far, index_far))):
+            first = (step * 2 + side) * capacity
+            for k in range(capacity):
+                page[first + k] = 0
+                count[first + k] = 0
+            base = (column ^ side) * slots
+
+            def visit(slot, found):
+                here = table[rank, slot] == me
+
+                @pl.when(here)
+                def _():
+                    page[first + found] = index[rank, slot]
+                    start = ((base + slot) % PAGES) * PAGE
+                    count[first + found] = jnp.clip(length - start, 0, PAGE)
+
+                return found + here.astype(jnp.int32)
+
+            lax.fori_loop(0, slots, visit, 0)
+
+
+def attend_kernel(capacity, heads, place, page, count, *refs):
+    ranks = (len(refs) - 4) // 2
+    query_refs, (near, far, fresh) = refs[:ranks], refs[ranks : ranks + 3]
+    out_refs, held = refs[ranks + 3 : -1], refs[-1]
+    me, column = place[0], place[1]
+    rows = query_refs[0].shape[0]
+    steps = rows // (ranks * heads)
+    lanes = lane_ids(rows)
+    across = (((1,), (1,)), ((), ()))
+    for step in range(ranks):
+        rank = me ^ step
+        query = query_refs[step][...]
+        scores, values = [], []
+        for side, pages in enumerate((near, far)):
+            for k in range(capacity):
+                place_of = (step * 2 + side) * capacity + k
+                keys = pages.at[page[place_of]]
+                score = jnp.dot(query, keys[...], preferred_element_type=jnp.float32) * score_scale
+                scores.append(jnp.where(lanes < count[place_of], score, mask_value))
+                values.append(keys)
+        peak = functools.reduce(jnp.maximum, scores)
+        row_peak = jnp.max(peak, axis=1, keepdims=True)
+        if step == 0:
+            recent = lax.dot_general(
+                query, fresh[...], across, preferred_element_type=jnp.float32
+            ) * score_scale
+            width = recent.shape[1]
+            key = lax.broadcasted_iota(jnp.int32, (rows, width), 1)
+            row_step = lax.broadcasted_iota(jnp.int32, (rows, width), 0) // (ranks * heads)
+            seen = (key <= row_step) & (column < 2)
+            recent = jnp.where(seen, recent, mask_value)
+            row_peak = jnp.maximum(row_peak, jnp.max(recent, axis=1, keepdims=True))
+        total, summed = None, None
+        for score, keys in zip(scores, values):
+            weight = jnp.where(score > 0.5 * mask_value, jnp.exp(score - row_peak), 0.0)
+            total = weight if total is None else total + weight
+            part = lax.dot_general(
+                weight.astype(jnp.bfloat16), keys[0:CKV, :], across, preferred_element_type=jnp.float32
+            )
+            summed = part if summed is None else summed + part
+        row_total = jnp.sum(total, axis=1, keepdims=True)
+        if step == 0:
+            weight = jnp.where(seen, jnp.exp(recent - row_peak), 0.0)
+            row_total = row_total + jnp.sum(weight, axis=1, keepdims=True)
+            summed = summed + jnp.dot(
+                weight.astype(jnp.bfloat16), fresh[:, 0:CKV], preferred_element_type=jnp.float32
+            )
+        extra = jnp.zeros((rows, LANES), jnp.float32)
+        for lane, part in enumerate(thirds(row_peak) + thirds(row_total)):
+            extra = jnp.where(lanes == lane, part, extra)
+        held[:, 0:CKV] = summed
+        held[:, CKV:] = extra
+        for far_step, out in enumerate(out_refs):
+            target = me ^ far_step
+            block = [
+                held[pl.ds(pl.multiple_of((u * ranks + target) * heads, heads), heads), :]
+                for u in range(steps)
+            ]
+            start = pl.multiple_of(rank * steps * heads, steps * heads)
+            out[pl.ds(start, steps * heads), :] = jnp.concatenate(block, axis=0).astype(jnp.bfloat16)
+
+
+def lift_kernel(heads, ranks, place, *refs):
+    parts, up_value, out, joined, tall = refs[:ranks], refs[ranks], refs[ranks + 1], refs[-2], refs[-1]
+    count = parts[0].shape[0]
+    rows = count // heads
+    core = place[1] % 2
+    blocks = [part[...].astype(jnp.float32) for part in parts]
+    peaks = [b[:, CKV : CKV + 1] + b[:, CKV + 1 : CKV + 2] + b[:, CKV + 2 : CKV + 3] for b in blocks]
+    totals = [b[:, CKV + 3 : CKV + 4] + b[:, CKV + 4 : CKV + 5] + b[:, CKV + 5 : CKV + 6] for b in blocks]
+    peak = functools.reduce(jnp.maximum, peaks)
+    value, total = 0.0, 0.0
+    for block, own_peak, own_total in zip(blocks, peaks, totals):
+        factor = jnp.exp(own_peak - peak)
+        value = value + block[:, 0:CKV] * factor
+        total = total + own_total * factor
+    for group in range(CKV // LANES):
+        joined[group] = value[:, group * LANES : (group + 1) * LANES]
+    lanes = lane_ids(count)
+    tall[...] = jnp.where(lanes < 3 * heads, peak, total)
+    lanes = lane_ids(rows)
+    extra = jnp.zeros((rows, LANES), jnp.float32)
+    for head in range(heads):
+        pick = pl.ds(head, rows, stride=heads)
+        out[:, head * LANES : (head + 1) * LANES] = jnp.dot(
+            jnp.concatenate([joined[g, pick, :] for g in range(CKV // LANES)], axis=1).astype(jnp.bfloat16),
+            up_value[core * heads + head],
+            preferred_element_type=jnp.float32,
+        ).astype(jnp.bfloat16)
+        extra = jnp.where(lanes % heads == head, tall[pick, :], extra)
+    high, middle, low = thirds(extra)
+    piece = lanes // heads % 3
+    out[:, heads * LANES :] = jnp.where(
+        piece == 0, high, jnp.where(piece == 1, middle, low)
+    ).astype(jnp.bfloat16)
+
+
+def project_kernel(heads, reps, place, *refs):
+    parts, (out_proj, own_rows, sent, kept) = refs[:reps], refs[reps:]
+    core = place[1] % 2
+    width = heads * LANES
+    result = own_rows[...]
+    for side in range(2):
+        blocks = [parts[step][...].astype(jnp.float32) for step in range(side, reps, 2)]
+        tails = [b[:, width:] for b in blocks]
+
+        def whole(tail, first):
+            at = [pltpu.roll(tail, LANES - (first + k) * heads, 1) if first + k else tail for k in range(3)]
+            return at[0] + at[1] + at[2]
+
+        peaks = [whole(tail, 0) for tail in tails]
+        totals = [whole(tail, 3) for tail in tails]
+        live = lane_ids(result.shape[0]) < heads
+        peaks = [jnp.where(live, p, 0.0) for p in peaks]
+        totals = [jnp.where(live, t, 1.0) for t in totals]
+        peak = functools.reduce(jnp.maximum, peaks)
+        factors = [jnp.exp(p - peak) for p in peaks]
+        total = sum(f * t for f, t in zip(factors, totals))
+        factors = [f / total for f in factors]
+        mixed = []
+        for head in range(heads):
+            lane = slice(head * LANES, (head + 1) * LANES)
+            mixed.append(sum(b[:, lane] * f[:, head : head + 1] for b, f in zip(blocks, factors)))
+        values = jnp.concatenate(mixed, axis=1).astype(jnp.bfloat16)
+        start = pl.multiple_of((core ^ side) * width, width)
+        result = result + jnp.dot(
+            values, out_proj[pl.ds(start, width), :], preferred_element_type=jnp.float32
+        )
+    kept[...] = result
+    sent[...] = result.astype(jnp.bfloat16)
+
+
+def gate_kernel(ranks, *refs):
+    kept, others, (gain, w_gate, w_up, out, mixed_out) = refs[0], refs[1:ranks], refs[ranks:]
+    mixed = kept[...]
+    for other in others:
+        mixed = mixed + other[...].astype(jnp.float32)
+    mixed_out[...] = mixed
+    scaled = (mixed * gain[...]).astype(jnp.bfloat16)
+    width = w_gate.shape[1]
+    out[:, 0:width] = jnp.dot(scaled, w_gate[...], preferred_element_type=jnp.float32).astype(jnp.bfloat16)
+    out[:, width : 2 * width] = jnp.dot(scaled, w_up[...], preferred_element_type=jnp.float32).astype(
+        jnp.bfloat16
+    )
+    squares = jnp.sum(mixed * mixed, axis=1, keepdims=True)
+    lanes = lane_ids(mixed.shape[0])
+    extra = jnp.zeros(lanes.shape, jnp.float32)
+    for lane, part in enumerate(thirds(squares)):
+        extra = jnp.where(lanes == lane, part, extra)
+    out[:, 2 * width :] = extra.astype(jnp.bfloat16)
+
+
+def down_kernel(reps, model_width, *refs):
+    parts, (w_down, out) = refs[:reps], refs[reps:]
+    width = w_down.shape[0]
+    total = parts[0][...].astype(jnp.float32)
+    for part in parts[1:]:
+        total = total + part[...].astype(jnp.float32)
+    tail = total[:, 2 * width :]
+    squares = jnp.sum(jnp.where(lane_ids(tail.shape[0]) < 3, tail, 0.0), axis=1, keepdims=True)
+    scale = lax.rsqrt(squares / model_width + epsilon)
+    gate = total[:, 0:width] * scale
+    hidden = (jax.nn.silu(gate) * (total[:, width : 2 * width] * scale)).astype(jnp.bfloat16)
+    out[...] = jnp.dot(hidden, w_down[...], preferred_element_type=jnp.float32).astype(jnp.bfloat16)
+
+
+def call(kernel, name, operands, specs, outputs, limit, flops=0, moved=0, scratch=(), out_specs=None):
+    return pl.pallas_call(
+        kernel,
+        name=name,
+        out_shape=outputs,
+        in_specs=specs,
+        out_specs=jax.tree.map(lambda _: vmem(), outputs) if out_specs is None else out_specs,
+        scratch_shapes=list(scratch),
+        compiler_params=pltpu.CompilerParams(vmem_limit_bytes=limit),
+        cost_estimate=pl.CostEstimate(flops=flops, bytes_accessed=moved, transcendentals=0),
+    )(*operands)
+
+
+def shape_of(shape, dtype=jnp.bfloat16):
+    return jax.ShapeDtypeStruct(shape, dtype)
+
+
+def queries_moved(
+    latent_store,
+    page_rank,
+    page_index,
+    lengths,
+    queries,
+    new_latent,
+    up_value,
+    out_proj,
+    residual,
+    norm_gain,
+    w_gate,
+    w_up,
+    w_down,
+):
+    ranks, reps = lax.axis_size("dp"), lax.axis_size("rep")
+    me, column = lax.axis_index("dp"), lax.axis_index("rep")
+    slots = page_rank.shape[1]
+    capacity = (slots + ranks - 1) // ranks
+    steps, columns = residual.shape
+    latent = new_latent.shape[1]
+    head_count = queries.shape[1] // latent
+    heads = head_count // (2 * ranks)
+    rows = ranks * steps
+    core_pairs = [(i, i ^ 1) for i in range(reps)]
+    place = jnp.stack([me, column])
+
+    share = lax.dynamic_index_in_dim(
+        queries.reshape(steps, ranks, 2, heads * latent), column % 2, 2, keepdims=False
+    )
+    arrived = [share] + partners(share, "dp")
+    near = latent_store[0]
+    far = lax.ppermute(near, "rep", core_pairs)
+    tables = lax.ppermute(jnp.stack([page_rank, page_index]), "rep", core_pairs)
+    found = 2 * ranks * capacity
+    page, count = call(
+        functools.partial(locate_kernel, capacity, slots),
+        "locate",
+        (place, lengths, page_rank, page_index, tables[0], tables[1]),
+        [smem()] * 6,
+        [shape_of((found,), jnp.int32)] * 2,
+        4 * MIB,
+        out_specs=[smem()] * 2,
+    )
+    fresh = jnp.concatenate([new_latent, jnp.zeros((8 - steps, latent), new_latent.dtype)])
+    own_rows = jnp.where(
+        (jnp.arange(rows) // steps == me)[:, None], jnp.tile(residual.astype(jnp.float32), (ranks, 1)), 0.0
+    )
+    query_rows = [a.reshape(steps * ranks * heads, latent) for a in arrived]
+    width = CKV + LANES
+    partial_rows = call(
+        functools.partial(attend_kernel, capacity, heads),
+        "attend",
+        (place, page, count, *query_rows, near, far, fresh),
+        [smem()] * 3 + [vmem()] * (ranks + 3),
+        [shape_of((rows * heads, width))] * ranks,
+        12 * MIB,
+        scratch=[pltpu.VMEM((steps * ranks * heads, width), jnp.float32)],
+        flops=2 * 2 * slots * PAGE * rows * heads * latent,
+        moved=2 * near.size * 2,
+    )
+    joined = [partial_rows[0]] + [
+        lax.ppermute(partial_rows[s], "dp", [(i, i ^ s) for i in range(ranks)]) for s in range(1, ranks)
+    ]
+    lifted = call(
+        functools.partial(lift_kernel, heads, ranks),
+        "lift",
+        (place, *joined, up_value),
+        [smem()] + [vmem()] * (ranks + 1),
+        shape_of((rows, (heads + 1) * LANES)),
+        8 * MIB,
+        scratch=[
+            pltpu.VMEM((CKV // LANES, rows * heads, LANES), jnp.float32),
+            pltpu.VMEM((rows * heads, LANES), jnp.float32),
+        ],
+        flops=2 * rows * heads * CKV * LANES,
+        moved=up_value.size * 2,
+    )
+    sent, kept = call(
+        functools.partial(project_kernel, heads, reps),
+        "project",
+        (place, lifted, *partners(lifted, "rep"), out_proj, own_rows),
+        [smem()] + [vmem()] * (reps + 2),
+        [shape_of((rows, columns)), shape_of((rows, columns), jnp.float32)],
+        12 * MIB,
+        flops=2 * rows * out_proj.size,
+        moved=out_proj.size * 2,
+    )
+    gate_up, mixed = call(
+        functools.partial(gate_kernel, ranks),
+        "gate",
+        (kept, *partners(sent, "dp"), norm_gain.reshape(1, columns), w_gate, w_up),
+        [vmem()] * (ranks + 3),
+        [shape_of((rows, 2 * w_gate.shape[1] + LANES)), shape_of((rows, columns), jnp.float32)],
+        28 * MIB,
+        flops=4 * rows * w_gate.size,
+        moved=w_gate.size * 4,
+    )
+    down = call(
+        functools.partial(down_kernel, reps, columns * reps),
+        "down",
+        (gate_up, *partners(gate_up, "rep"), w_down),
+        [vmem()] * (reps + 1),
+        shape_of((rows, columns)),
+        16 * MIB,
+        flops=2 * rows * w_down.size,
+        moved=w_down.size * 2,
+    )
+
+    def mine(array):
+        return lax.dynamic_slice_in_dim(array, me * steps, steps).astype(jnp.float32)
+
+    return (mine(mixed) + sum(mine(a) for a in [down] + partners(down, "dp"))).astype(jnp.bfloat16)
+
+
+def on_device(*arrays):
+    ranks = lax.axis_size("dp")
+    lengths, queries, new_latent = arrays[3:6]
+    heads = queries.shape[1] // new_latent.shape[1]
+    if ranks <= 8 and heads % (16 * ranks) == 0 and lengths.shape[1] == 1:
+        return queries_moved(*arrays)
+    return pages_moved(*arrays)
 
 
 def solution(mesh):

time: 226 us -> 76.6 us (0.34)
  blocking collectives: 72.8 us -> 0 us
  waiting for transfers between devices: 74.9 us -> 22.5 us
  matrix products: 32.4 us -> 0 us
  between operations: 14.3 us -> 0.19 us
  Pallas kernels: 0 us -> 13.2 us
  starting transfers between devices: 9.85 us -> 23 us
  other arithmetic: 12.1 us -> 1.49 us
  local copies, waits for them, and re-layouts: 9.15 us -> 15.8 us
    all_to_all x2 -> x0, waiting for transfers between devices: 44.6 us -> none  [the longest x1 39.4 us: on_device(): lax.all_to_all(outgoing, 'dp', split_axis=0, concat_axis=0, tiled=True)]
    unnamed x2 -> x0, blocking collectives: 36.4 us -> none
    dot_general x9 -> x0, matrix products: 32.4 us -> none  [the longest x1 7.4 us: join_pages(): jnp.einsum('jpsh,pshc->jshc', factor, partial_value, precision=lax.Precis...]
    all_gather x4 -> x0, blocking collectives: 30.6 us -> none  [the longest x3 17.4 us: merged_2(): lax.all_gather(a.astype(kind), axis)]
    psum x1 -> x0, waiting for transfers between devices: 30.3 us -> none  [on_device(): lax.psum(partial_rows.astype(jnp.bfloat16), 'rep').astype(jnp.float32)]
    ppermute x0 -> x20, starting transfers between devices: none -> 23 us  [the longest x15 18.1 us: partners(): lax.ppermute(array, axis, [(i, i ^ step) for i in range(size)])]
    ppermute x0 -> x20, waiting for transfers between devices: none -> 22.5 us  [the longest x15 15.7 us: partners(): lax.ppermute(array, axis, [(i, i ^ step) for i in range(size)])]
    pallas_call x0 -> x6, Pallas kernels: none -> 13.2 us  [call(): pl.pallas_call(kernel, name=name, out_shape=outputs, in_specs=specs, out_...]
  transfers between devices with their start and end apart: 3 -> 20, of which waited for: 3 -> 10; matrix products, arithmetic and copies ran while one was open for 1% -> 6% of each run, Pallas kernels for 0% -> 4%
where the time goes in v1:
time: 76.6 us; the launch traced here: 76.2 us
  starting transfers between devices  23 us (30%)
  waiting for transfers between devices  22.5 us (29%)
  local copies, waits for them, and re-layouts  15.8 us (21%)
  Pallas kernels  13.2 us (17%)
  other arithmetic  1.49 us (2%)
    ppermute x15, starting transfers between devices, partners(): lax.ppermute(array, axis, [(i, i ^ step) for i in range(size)])  18.1 us
    ppermute x15, waiting for transfers between devices, partners(): lax.ppermute(array, axis, [(i, i ^ step) for i in range(size)])  15.7 us
    pallas_call x6, Pallas kernels, call(): pl.pallas_call(kernel, name=name, out_shape=outputs, in_specs=specs, out_...  13.2 us
    unnamed x21, local copies, waits for them, and re-layouts  12.6 us
    ppermute x3, waiting for transfers between devices, queries_moved(): lax.ppermute(partial_rows[s], 'dp', [(i, i ^ s) for i in range(ranks)])  6.79 us
    ppermute x3, starting transfers between devices, queries_moved(): lax.ppermute(partial_rows[s], 'dp', [(i, i ^ s) for i in range(ranks)])  4.46 us
  transfers between devices with their start and end apart: 20, of which 10 were waited for; matrix products, arithmetic and copies ran while one was open for 6% of the time, Pallas kernels for 4%

profile of v1, /device:TPU:0, one launch (start us, length us, event | category | flops | bytes accessed | tf_op | source)
XLA Modules:
  0.0 76.2 jit_solution(9074360370072726126)
XLA Ops:
  0.0 0.5 collective-permute-start.4
  0.5 1.0 %reshape.37 = bf16[2,4,2,4608]{3,2,1,0:T(2,128)(2,1)S(1)} reshape(bf16[2,36864]{1,0:T(2,128)(2,1)} %param.17) | data formatting | bytes 294912 | tf_op jit(solution)/shard_map/reshape | solution.py:461
  1.5 0.2 constant_dynamic-slice_fusion
  1.7 2.6 %collective-permute-start.1 = (bf16[2,4,4608]{2,1,0:T(4,128)(2,1)S(1)}, bf16[2,4,4608]{2,1,0:T(4,128)(2,1)S(1)}, u32[]{:S(2)}, u32[]{:S(2)}) collective-permute-start(bf16[2,4,4608]{2,1,0:T(4,128)(2,1)S(1)} %bitcast.18), channel_id=1, source_target_pairs={{0,4},{4,0},{8,12},{12,8},{1,5},{5,1},{9,13},{13,9},{2,6},{6,2},{1... | collective-permute-start | bytes 221192 | tf_op jit(solution)/shard_map/ppermute | solution.py:200
  4.4 2.6 %collective-permute-start.2 = (bf16[2,4,4608]{2,1,0:T(4,128)(2,1)S(1)}, bf16[2,4,4608]{2,1,0:T(4,128)(2,1)S(1)}, u32[]{:S(2)}, u32[]{:S(2)}) collective-permute-start(bf16[2,4,4608]{2,1,0:T(4,128)(2,1)S(1)} %bitcast.19), channel_id=1, source_target_pairs={{0,8},{4,12},{8,0},{12,4},{1,9},{5,13},{9,1},{13,5},{2,10},{6,14},... | collective-permute-start | bytes 221192 | tf_op jit(solution)/shard_map/ppermute | solution.py:200
  7.0 0.0 collective-permute-start.3
  7.0 0.7 pad_add_fusion
  7.7 0.0 collective-permute-start
  7.7 0.1 reshape.38.refs_0_
  7.8 0.0 copy-start.8
  7.9 0.1 pad_add_fusion.1.place
  7.9 0.7 copy.14.lengths
  8.7 0.7 tile.4
  9.4 0.7 concatenate.3.refs_6_
  10.1 0.0 copy-start.6
  10.2 0.7 copy-done.6
  10.8 0.7 copy-done.7
  11.5 2.7 %locate.1 = (s32[24]{0:T(128)S(1)}, s32[24]{0:T(128)S(1)}) custom-call(s32[2]{0:T(128)S(1)} %pad_add_fusion.1.place, s32[4,1]{1,0:T(4,128)S(1)} %copy.14.lengths, s32[4,12]{1,0:T(4,128)S(1)} %copy-done.6, s32[4,12]{1,0:T(4,128)S(1)} %copy-done.7, s32[4,12]{1,0:T(4,128)S(1)} %get-tuple-element.26.rank_far, s32[4,12]{1,0:T(4,128)S(1)} %get-tuple-element.25.index_far), custom_call_target="tpu_custom_call" | custom-call | tf_op jit(solution)/shard_map/locate/pallas_call | solution.py:417
  14.3 0.0 collective-permute-done.1
  14.3 0.1 reshape.39.refs_1_
  14.4 0.0 collective-permute-done.2
  14.4 0.1 reshape.40.refs_2_
  14.5 0.0 collective-permute-done.3
  14.5 0.1 reshape.41.refs_3_
  14.7 0.0 copy-start
  14.7 0.0 collective-permute-done.4.refs_5_
  14.7 0.0 copy-start.5
  14.7 1.6 %copy-done.5 = bf16[1,12,576,128]{3,2,1,0:T(8,128)(2,1)S(1)} copy-done((bf16[1,12,576,128]{3,2,1,0:T(8,128)(2,1)S(1)}, bf16[1,12,576,128]{3,2,1,0:T(8,128)(2,1)}, u32[]{:S(2)}) %copy-start.5) | copy-done | bytes 1769496
  16.3 3.2 %attend.1 = (bf16[64,640]{1,0:T(8,128)(2,1)S(1)}, bf16[64,640]{1,0:T(8,128)(2,1)S(1)}, bf16[64,640]{1,0:T(8,128)(2,1)S(1)}, bf16[64,640]{1,0:T(8,128)(2,1)S(1)}) custom-call(s32[2]{0:T(128)S(1)} %pad_add_fusion.1.place, s32[24]{0:T(128)S(1)} %get-tuple-element.15.page, s32[24]{0:T(128)S(1)} %get-tuple-element.16.count, bf16[64,576]{1,0:T(8,128)(2,1)S(1)} %reshape.38.refs_0_, ...), custom_call_target="tpu_custom_call" | custom-call | flops 226492416 | bytes 3538944 | tf_op jit(solution)/shard_map/attend/pallas_call | solution.py:417
  19.5 1.0 %collective-permute-start.5 = (bf16[64,640]{1,0:T(8,128)(2,1)S(1)}, bf16[64,640]{1,0:T(8,128)(2,1)S(1)}, u32[]{:S(2)}, u32[]{:S(2)}) collective-permute-start(bf16[64,640]{1,0:T(8,128)(2,1)S(1)} %get-tuple-element.18), channel_id=1, source_target_pairs={{0,4},{4,0},{8,12},{12,8},{1,5},{5,1},{9,13},{13,9},{2,6},{6,2},{1... | collective-permute-start | bytes 245768 | tf_op jit(solution)/shard_map/ppermute | solution.py:495
  20.5 3.5 %collective-permute-start.6 = (bf16[64,640]{1,0:T(8,128)(2,1)S(1)}, bf16[64,640]{1,0:T(8,128)(2,1)S(1)}, u32[]{:S(2)}, u32[]{:S(2)}) collective-permute-start(bf16[64,640]{1,0:T(8,128)(2,1)S(1)} %get-tuple-element.19), channel_id=1, source_target_pairs={{0,8},{4,12},{8,0},{12,4},{1,9},{5,13},{9,1},{13,5},{2,10},{6,14},... | collective-permute-start | bytes 245768 | tf_op jit(solution)/shard_map/ppermute | solution.py:495
  24.0 0.5 collective-permute-done.5.refs_1_
  24.5 6.3 %collective-permute-done.6.refs_2_ = bf16[64,640]{1,0:T(8,128)(2,1)S(1)} collective-permute-done((bf16[64,640]{1,0:T(8,128)(2,1)S(1)}, bf16[64,640]{1,0:T(8,128)(2,1)S(1)}, u32[]{:S(2)}, u32[]{:S(2)}) %collective-permute-start.6) | collective-permute-done | bytes 81952 | tf_op jit(solution)/shard_map/ppermute | solution.py:495
  30.8 1.6 %copy-done.4 = bf16[16,512,128]{2,1,0:T(8,128)(2,1)S(1)} copy-done((bf16[16,512,128]{2,1,0:T(8,128)(2,1)S(1)}, bf16[16,512,128]{2,1,0:T(8,128)(2,1)}, u32[]{:S(2)}) %copy-start.4) | copy-done | bytes 2097176
  32.4 1.0 %lift.1.refs_0_ = bf16[8,1152]{1,0:T(8,128)(2,1)S(1)} custom-call(s32[2]{0:T(128)S(1)} %pad_add_fusion.1.place, bf16[64,640]{1,0:T(8,128)(2,1)S(1)} %get-tuple-element.17.refs_0_, bf16[64,640]{1,0:T(8,128)(2,1)S(1)} %collective-permute-done.5.refs_1_, bf16[64,640]{1,0:T(8,128)(2,1)S(1)} %collective-permute-done.6.refs_2_, ...), custom_call_target="tpu_custom_call" | custom-call | flops 8388608 | bytes 2097152 | tf_op jit(solution)/shard_map/lift/pallas_call | solution.py:417
  33.4 0.1 collective-permute-start.10
  33.5 1.6 %collective-permute-start.8 = (bf16[8,1152]{1,0:T(8,128)(2,1)S(1)}, bf16[8,1152]{1,0:T(8,128)(2,1)S(1)}, u32[]{:S(2)}, u32[]{:S(2)}) collective-permute-start(bf16[8,1152]{1,0:T(8,128)(2,1)S(1)} %lift.1.refs_0_), channel_id=1, source_target_pairs={{0,1},{1,0},{2,3},{3,2},{4,5},{5,4},{6,7},{7,6},{8,9},{9,8},{10,11... | collective-permute-start | bytes 55304 | tf_op jit(solution)/shard_map/ppermute | solution.py:200
  35.1 0.5 collective-permute-start.9
  35.6 0.1 broadcast_select_fusion.refs_5_
  35.7 1.1 %collective-permute-done.10.refs_3_ = bf16[8,1152]{1,0:T(8,128)(2,1)S(1)} collective-permute-done((bf16[8,1152]{1,0:T(8,128)(2,1)S(1)}, bf16[8,1152]{1,0:T(8,128)(2,1)S(1)}, u32[]{:S(2)}, u32[]{:S(2)}) %collective-permute-start.10) | collective-permute-done | bytes 18464 | tf_op jit(solution)/shard_map/ppermute | solution.py:200
  36.8 0.0 collective-permute-done.8.refs_1_
  36.8 2.0 %collective-permute-done.9.refs_2_ = bf16[8,1152]{1,0:T(8,128)(2,1)S(1)} collective-permute-done((bf16[8,1152]{1,0:T(8,128)(2,1)S(1)}, bf16[8,1152]{1,0:T(8,128)(2,1)S(1)}, u32[]{:S(2)}, u32[]{:S(2)}) %collective-permute-start.9) | collective-permute-done | bytes 18464 | tf_op jit(solution)/shard_map/ppermute | solution.py:200
  38.8 3.1 %copy-done.3 = bf16[2048,1792]{1,0:T(8,128)(2,1)S(1)} copy-done((bf16[2048,1792]{1,0:T(8,128)(2,1)S(1)}, bf16[2048,1792]{1,0:T(8,128)(2,1)}, u32[]{:S(2)}) %copy-start.3) | copy-done | bytes 7340056
  41.9 1.7 %project.1 = (bf16[8,1792]{1,0:T(8,128)(2,1)S(1)}, f32[8,1792]{1,0:T(8,128)S(1)}) custom-call(s32[2]{0:T(128)S(1)} %pad_add_fusion.1.place, bf16[8,1152]{1,0:T(8,128)(2,1)S(1)} %lift.1.refs_0_, bf16[8,1152]{1,0:T(8,128)(2,1)S(1)} %collective-permute-done.8.refs_1_, bf16[8,1152]{1,0:T(8,128)(2,1)S(1)} %collective-permute-done.9.refs_2_, ...), custom_call_target="tpu_custom_call" | custom-call | flops 58720256 | bytes 7340032 | tf_op jit(solution)/shard_map/project/pallas_call | solution.py:417
  43.6 1.9 %collective-permute-start.11 = (bf16[8,1792]{1,0:T(8,128)(2,1)S(1)}, bf16[8,1792]{1,0:T(8,128)(2,1)S(1)}, u32[]{:S(2)}, u32[]{:S(2)}) collective-permute-start(bf16[8,1792]{1,0:T(8,128)(2,1)S(1)} %get-tuple-element.22), channel_id=1, source_target_pairs={{0,4},{4,0},{8,12},{12,8},{1,5},{5,1},{9,13},{13,9},{2,6},{6,2},{1... | collective-permute-start | bytes 86024 | tf_op jit(solution)/shard_map/ppermute | solution.py:200
  45.5 1.2 %collective-permute-start.12 = (bf16[8,1792]{1,0:T(8,128)(2,1)S(1)}, bf16[8,1792]{1,0:T(8,128)(2,1)S(1)}, u32[]{:S(2)}, u32[]{:S(2)}) collective-permute-start(bf16[8,1792]{1,0:T(8,128)(2,1)S(1)} %get-tuple-element.22), channel_id=1, source_target_pairs={{0,8},{4,12},{8,0},{12,4},{1,9},{5,13},{9,1},{13,5},{2,10},{6,14},... | collective-permute-start | bytes 86024 | tf_op jit(solution)/shard_map/ppermute | solution.py:200
  46.7 1.3 %collective-permute-start.13 = (bf16[8,1792]{1,0:T(8,128)(2,1)S(1)}, bf16[8,1792]{1,0:T(8,128)(2,1)S(1)}, u32[]{:S(2)}, u32[]{:S(2)}) collective-permute-start(bf16[8,1792]{1,0:T(8,128)(2,1)S(1)} %get-tuple-element.22), channel_id=1, source_target_pairs={{0,12},{4,8},{8,4},{12,0},{1,13},{5,9},{9,5},{13,1},{2,14},{6,10},... | collective-permute-start | bytes 86024 | tf_op jit(solution)/shard_map/ppermute | solution.py:200
  48.1 2.6 %collective-permute-done.12.refs_2_ = bf16[8,1792]{1,0:T(8,128)(2,1)S(1)} collective-permute-done((bf16[8,1792]{1,0:T(8,128)(2,1)S(1)}, bf16[8,1792]{1,0:T(8,128)(2,1)S(1)}, u32[]{:S(2)}, u32[]{:S(2)}) %collective-permute-start.12) | collective-permute-done | bytes 28704 | tf_op jit(solution)/shard_map/ppermute | solution.py:200
  50.7 1.7 %collective-permute-done.13.refs_3_ = bf16[8,1792]{1,0:T(8,128)(2,1)S(1)} collective-permute-done((bf16[8,1792]{1,0:T(8,128)(2,1)S(1)}, bf16[8,1792]{1,0:T(8,128)(2,1)S(1)}, u32[]{:S(2)}, u32[]{:S(2)}) %collective-permute-start.13) | collective-permute-done | bytes 28704 | tf_op jit(solution)/shard_map/ppermute | solution.py:200
  52.4 4.1 %copy-done.1 = bf16[1792,3072]{1,0:T(8,128)(2,1)S(1)} copy-done((bf16[1792,3072]{1,0:T(8,128)(2,1)S(1)}, bf16[1792,3072]{1,0:T(8,128)(2,1)}, u32[]{:S(2)}) %copy-start.1) | copy-done | bytes 11010072
  56.5 3.0 %gate.1 = (bf16[8,6272]{1,0:T(8,128)(2,1)S(1)}, f32[8,1792]{1,0:T(8,128)S(1)}) custom-call(f32[8,1792]{1,0:T(8,128)S(1)} %get-tuple-element.21.refs_0_, bf16[8,1792]{1,0:T(8,128)(2,1)S(1)} %collective-permute-done.11.refs_1_, bf16[8,1792]{1,0:T(8,128)(2,1)S(1)} %collective-permute-done.12.refs_2_, bf16[8,1792]{1,0:T(8,128)(2,1)S(1)} %collective-permute-done.13.refs_3_, ...), custom_call_target="tpu_custom_call" | custom-call | flops 176160768 | bytes 22020096 | tf_op jit(solution)/shard_map/gate/pallas_call | solution.py:417
  59.5 0.0 collective-permute-start.14
  59.5 0.6 collective-permute-start.15
  60.1 1.3 %collective-permute-start.16 = (bf16[8,6272]{1,0:T(8,128)(2,1)S(1)}, bf16[8,6272]{1,0:T(8,128)(2,1)S(1)}, u32[]{:S(2)}, u32[]{:S(2)}) collective-permute-start(bf16[8,6272]{1,0:T(8,128)(2,1)S(1)} %get-tuple-element.24.refs_0_), channel_id=1, source_target_pairs={{0,3},{1,2},{2,1},{3,0},{4,7},{5,6},{6,5},{7,4},{8,11},{9,10},{10,... | collective-permute-start | bytes 301064 | tf_op jit(solution)/shard_map/ppermute | solution.py:200
  61.3 0.0 collective-permute-done.14.refs_1_
  61.3 3.9 %collective-permute-done.15.refs_2_ = bf16[8,6272]{1,0:T(8,128)(2,1)S(1)} collective-permute-done((bf16[8,6272]{1,0:T(8,128)(2,1)S(1)}, bf16[8,6272]{1,0:T(8,128)(2,1)S(1)}, u32[]{:S(2)}, u32[]{:S(2)}) %collective-permute-start.15) | collective-permute-done | bytes 100384 | tf_op jit(solution)/shard_map/ppermute | solution.py:200
  65.2 1.1 %collective-permute-done.16.refs_3_ = bf16[8,6272]{1,0:T(8,128)(2,1)S(1)} collective-permute-done((bf16[8,6272]{1,0:T(8,128)(2,1)S(1)}, bf16[8,6272]{1,0:T(8,128)(2,1)S(1)}, u32[]{:S(2)}, u32[]{:S(2)}) %collective-permute-start.16) | collective-permute-done | bytes 100384 | tf_op jit(solution)/shard_map/ppermute | solution.py:200
  66.4 1.6 %down.1 = bf16[8,1792]{1,0:T(8,128)(2,1)S(1)} custom-call(bf16[8,6272]{1,0:T(8,128)(2,1)S(1)} %get-tuple-element.24.refs_0_, bf16[8,6272]{1,0:T(8,128)(2,1)S(1)} %collective-permute-done.14.refs_1_, bf16[8,6272]{1,0:T(8,128)(2,1)S(1)} %collective-permute-done.15.refs_2_, bf16[8,6272]{1,0:T(8,128)(2,1)S(1)} %collective-permute-done.16.refs_3_, ...), custom_call_target="tpu_custom_call" | custom-call | flops 88080384 | bytes 11010048 | tf_op jit(solution)/shard_map/down/pallas_call | solution.py:417
  68.0 0.1 collective-permute-start.17
  68.0 1.8 %collective-permute-start.18 = (bf16[8,1792]{1,0:T(8,128)(2,1)S(1)}, bf16[8,1792]{1,0:T(8,128)(2,1)S(1)}, u32[]{:S(2)}, u32[]{:S(2)}) collective-permute-start(bf16[8,1792]{1,0:T(8,128)(2,1)S(1)} %down.1), channel_id=1, source_target_pairs={{0,8},{4,12},{8,0},{12,4},{1,9},{5,13},{9,1},{13,5},{2,10},{6,14},... | collective-permute-start | bytes 86024 | tf_op jit(solution)/shard_map/ppermute | solution.py:200
  69.9 2.5 %collective-permute-start.19 = (bf16[8,1792]{1,0:T(8,128)(2,1)S(1)}, bf16[8,1792]{1,0:T(8,128)(2,1)S(1)}, u32[]{:S(2)}, u32[]{:S(2)}) collective-permute-start(bf16[8,1792]{1,0:T(8,128)(2,1)S(1)} %down.1), channel_id=1, source_target_pairs={{0,12},{4,8},{8,4},{12,0},{1,13},{5,9},{9,5},{13,1},{2,14},{6,10},... | collective-permute-start | bytes 86024 | tf_op jit(solution)/shard_map/ppermute | solution.py:200
  72.4 0.4 collective-permute-done.18
  72.8 2.7 %collective-permute-done.19 = bf16[8,1792]{1,0:T(8,128)(2,1)S(1)} collective-permute-done((bf16[8,1792]{1,0:T(8,128)(2,1)S(1)}, bf16[8,1792]{1,0:T(8,128)(2,1)S(1)}, u32[]{:S(2)}, u32[]{:S(2)}) %collective-permute-start.19) | collective-permute-done | bytes 28704 | tf_op jit(solution)/shard_map/ppermute | solution.py:200
  75.6 0.6 add_convert_fusion
  (19 shorter events, 0.2 us)
Async XLA Ops:
  0.0 14.7 %collective-permute-start.4 = (bf16[12,576,128]{2,1,0:T(8,128)(2,1)}, bf16[12,576,128]{2,1,0:T(8,128)(2,1)S(1)}, u32[]{:S(2)}, u32[]{:S(2)}) collective-permute-start(bf16[12,576,128]{2,1,0:T(8,128)(2,1)} %bitcast.14), channel_id=1, source_target_pairs={{0,1},{1,0},{2,3},{3,2},{4,5},{5,4},{6,7},{7,6},{8,9},{9,8},{10,11... | collective-permute-start | bytes 5308424 | tf_op jit(solution)/shard_map/ppermute | solution.py:465
  1.7 12.5 %collective-permute-start.1 = (bf16[2,4,4608]{2,1,0:T(4,128)(2,1)S(1)}, bf16[2,4,4608]{2,1,0:T(4,128)(2,1)S(1)}, u32[]{:S(2)}, u32[]{:S(2)}) collective-permute-start(bf16[2,4,4608]{2,1,0:T(4,128)(2,1)S(1)} %bitcast.18), channel_id=1, source_target_pairs={{0,4},{4,0},{8,12},{12,8},{1,5},{5,1},{9,13},{13,9},{2,6},{6,2},{1... | collective-permute-start | bytes 221192 | tf_op jit(solution)/shard_map/ppermute | solution.py:200
  4.4 10.0 %collective-permute-start.2 = (bf16[2,4,4608]{2,1,0:T(4,128)(2,1)S(1)}, bf16[2,4,4608]{2,1,0:T(4,128)(2,1)S(1)}, u32[]{:S(2)}, u32[]{:S(2)}) collective-permute-start(bf16[2,4,4608]{2,1,0:T(4,128)(2,1)S(1)} %bitcast.19), channel_id=1, source_target_pairs={{0,8},{4,12},{8,0},{12,4},{1,9},{5,13},{9,1},{13,5},{2,10},{6,14},... | collective-permute-start | bytes 221192 | tf_op jit(solution)/shard_map/ppermute | solution.py:200
  7.0 7.6 %collective-permute-start.3 = (bf16[2,4,4608]{2,1,0:T(4,128)(2,1)S(1)}, bf16[2,4,4608]{2,1,0:T(4,128)(2,1)S(1)}, u32[]{:S(2)}, u32[]{:S(2)}) collective-permute-start(bf16[2,4,4608]{2,1,0:T(4,128)(2,1)S(1)} %bitcast.20), channel_id=1, source_target_pairs={{0,12},{4,8},{8,4},{12,0},{1,13},{5,9},{9,5},{13,1},{2,14},{6,10},... | collective-permute-start | bytes 221192 | tf_op jit(solution)/shard_map/ppermute | solution.py:200
  7.7 2.5 %collective-permute-start = (s32[2,4,12]{2,1,0:T(4,128)S(1)}, s32[2,4,12]{2,1,0:T(4,128)S(1)}, u32[]{:S(2)}, u32[]{:S(2)}) collective-permute-start(s32[2,4,12]{2,1,0:T(4,128)S(1)} %pad_add_fusion), channel_id=1, source_target_pairs={{0,1},{1,0},{2,3},{3,2},{4,5},{5,4},{6,7},{7,6},{8,9},{9,8},{10,11... | collective-permute-start | bytes 1160 | tf_op jit(solution)/shard_map/ppermute | solution.py:466
  7.8 40.2 %copy-start.8 = (f32[1792]{0:T(1024)S(1)}, f32[1792]{0:T(1024)}, u32[]{:S(2)}) copy-start(f32[1792]{0:T(1024)} %param.22) | copy-start | bytes 21508
  10.1 0.7 copy-start.6
  10.8 0.7 copy-start.7
  14.7 37.7 %copy-start = (bf16[1792,3072]{1,0:T(8,128)(2,1)S(1)}, bf16[1792,3072]{1,0:T(8,128)(2,1)}, u32[]{:S(2)}) copy-start(bf16[1792,3072]{1,0:T(8,128)(2,1)} %refs_5_.1) | copy-start | bytes 33030148
  14.7 1.6 %copy-start.5 = (bf16[1,12,576,128]{3,2,1,0:T(8,128)(2,1)S(1)}, bf16[1,12,576,128]{3,2,1,0:T(8,128)(2,1)}, u32[]{:S(2)}) copy-start(bf16[1,12,576,128]{3,2,1,0:T(8,128)(2,1)} %param.13) | copy-start | bytes 5308420
  19.5 4.9 %collective-permute-start.5 = (bf16[64,640]{1,0:T(8,128)(2,1)S(1)}, bf16[64,640]{1,0:T(8,128)(2,1)S(1)}, u32[]{:S(2)}, u32[]{:S(2)}) collective-permute-start(bf16[64,640]{1,0:T(8,128)(2,1)S(1)} %get-tuple-element.18), channel_id=1, source_target_pairs={{0,4},{4,0},{8,12},{12,8},{1,5},{5,1},{9,13},{13,9},{2,6},{6,2},{1... | collective-permute-start | bytes 245768 | tf_op jit(solution)/shard_map/ppermute | solution.py:495
  20.5 10.3 %collective-permute-start.6 = (bf16[64,640]{1,0:T(8,128)(2,1)S(1)}, bf16[64,640]{1,0:T(8,128)(2,1)S(1)}, u32[]{:S(2)}, u32[]{:S(2)}) collective-permute-start(bf16[64,640]{1,0:T(8,128)(2,1)S(1)} %get-tuple-element.19), channel_id=1, source_target_pairs={{0,8},{4,12},{8,0},{12,4},{1,9},{5,13},{9,1},{13,5},{2,10},{6,14},... | collective-permute-start | bytes 245768 | tf_op jit(solution)/shard_map/ppermute | solution.py:495
  24.0 6.8 %collective-permute-start.7 = (bf16[64,640]{1,0:T(8,128)(2,1)S(1)}, bf16[64,640]{1,0:T(8,128)(2,1)S(1)}, u32[]{:S(2)}, u32[]{:S(2)}) collective-permute-start(bf16[64,640]{1,0:T(8,128)(2,1)S(1)} %get-tuple-element.20), channel_id=1, source_target_pairs={{0,12},{4,8},{8,4},{12,0},{1,13},{5,9},{9,5},{13,1},{2,14},{6,10},... | collective-permute-start | bytes 245768 | tf_op jit(solution)/shard_map/ppermute | solution.py:495
  30.8 1.6 %copy-start.4 = (bf16[16,512,128]{2,1,0:T(8,128)(2,1)S(1)}, bf16[16,512,128]{2,1,0:T(8,128)(2,1)}, u32[]{:S(2)}) copy-start(bf16[16,512,128]{2,1,0:T(8,128)(2,1)} %refs_4_.3) | copy-start | bytes 6291460
  33.4 3.4 %collective-permute-start.10 = (bf16[8,1152]{1,0:T(8,128)(2,1)S(1)}, bf16[8,1152]{1,0:T(8,128)(2,1)S(1)}, u32[]{:S(2)}, u32[]{:S(2)}) collective-permute-start(bf16[8,1152]{1,0:T(8,128)(2,1)S(1)} %lift.1.refs_0_), channel_id=1, source_target_pairs={{0,3},{1,2},{2,1},{3,0},{4,7},{5,6},{6,5},{7,4},{8,11},{9,10},{10,... | collective-permute-start | bytes 55304 | tf_op jit(solution)/shard_map/ppermute | solution.py:200
  33.5 3.3 %collective-permute-start.8 = (bf16[8,1152]{1,0:T(8,128)(2,1)S(1)}, bf16[8,1152]{1,0:T(8,128)(2,1)S(1)}, u32[]{:S(2)}, u32[]{:S(2)}) collective-permute-start(bf16[8,1152]{1,0:T(8,128)(2,1)S(1)} %lift.1.refs_0_), channel_id=1, source_target_pairs={{0,1},{1,0},{2,3},{3,2},{4,5},{5,4},{6,7},{7,6},{8,9},{9,8},{10,11... | collective-permute-start | bytes 55304 | tf_op jit(solution)/shard_map/ppermute | solution.py:200
  35.1 3.8 %collective-permute-start.9 = (bf16[8,1152]{1,0:T(8,128)(2,1)S(1)}, bf16[8,1152]{1,0:T(8,128)(2,1)S(1)}, u32[]{:S(2)}, u32[]{:S(2)}) collective-permute-start(bf16[8,1152]{1,0:T(8,128)(2,1)S(1)} %lift.1.refs_0_), channel_id=1, source_target_pairs={{0,2},{1,3},{2,0},{3,1},{4,6},{5,7},{6,4},{7,5},{8,10},{9,11},{10,... | collective-permute-start | bytes 55304 | tf_op jit(solution)/shard_map/ppermute | solution.py:200
  38.8 3.1 %copy-start.3 = (bf16[2048,1792]{1,0:T(8,128)(2,1)S(1)}, bf16[2048,1792]{1,0:T(8,128)(2,1)}, u32[]{:S(2)}) copy-start(bf16[2048,1792]{1,0:T(8,128)(2,1)} %refs_4_.4) | copy-start | bytes 22020100
  43.6 4.4 %collective-permute-start.11 = (bf16[8,1792]{1,0:T(8,128)(2,1)S(1)}, bf16[8,1792]{1,0:T(8,128)(2,1)S(1)}, u32[]{:S(2)}, u32[]{:S(2)}) collective-permute-start(bf16[8,1792]{1,0:T(8,128)(2,1)S(1)} %get-tuple-element.22), channel_id=1, source_target_pairs={{0,4},{4,0},{8,12},{12,8},{1,5},{5,1},{9,13},{13,9},{2,6},{6,2},{1... | collective-permute-start | bytes 86024 | tf_op jit(solution)/shard_map/ppermute | solution.py:200
  45.5 5.2 %collective-permute-start.12 = (bf16[8,1792]{1,0:T(8,128)(2,1)S(1)}, bf16[8,1792]{1,0:T(8,128)(2,1)S(1)}, u32[]{:S(2)}, u32[]{:S(2)}) collective-permute-start(bf16[8,1792]{1,0:T(8,128)(2,1)S(1)} %get-tuple-element.22), channel_id=1, source_target_pairs={{0,8},{4,12},{8,0},{12,4},{1,9},{5,13},{9,1},{13,5},{2,10},{6,14},... | collective-permute-start | bytes 86024 | tf_op jit(solution)/shard_map/ppermute | solution.py:200
  46.7 5.7 %collective-permute-start.13 = (bf16[8,1792]{1,0:T(8,128)(2,1)S(1)}, bf16[8,1792]{1,0:T(8,128)(2,1)S(1)}, u32[]{:S(2)}, u32[]{:S(2)}) collective-permute-start(bf16[8,1792]{1,0:T(8,128)(2,1)S(1)} %get-tuple-element.22), channel_id=1, source_target_pairs={{0,12},{4,8},{8,4},{12,0},{1,13},{5,9},{9,5},{13,1},{2,14},{6,10},... | collective-permute-start | bytes 86024 | tf_op jit(solution)/shard_map/ppermute | solution.py:200
  52.4 4.1 %copy-start.1 = (bf16[1792,3072]{1,0:T(8,128)(2,1)S(1)}, bf16[1792,3072]{1,0:T(8,128)(2,1)}, u32[]{:S(2)}) copy-start(bf16[1792,3072]{1,0:T(8,128)(2,1)} %refs_6_.1) | copy-start | bytes 33030148
  56.5 9.9 %copy-start.2 = (bf16[3072,1792]{1,0:T(8,128)(2,1)S(1)}, bf16[3072,1792]{1,0:T(8,128)(2,1)}, u32[]{:S(2)}) copy-start(bf16[3072,1792]{1,0:T(8,128)(2,1)} %refs_4_.5) | copy-start | bytes 33030148
  59.5 1.9 %collective-permute-start.14 = (bf16[8,6272]{1,0:T(8,128)(2,1)S(1)}, bf16[8,6272]{1,0:T(8,128)(2,1)S(1)}, u32[]{:S(2)}, u32[]{:S(2)}) collective-permute-start(bf16[8,6272]{1,0:T(8,128)(2,1)S(1)} %get-tuple-element.24.refs_0_), channel_id=1, source_target_pairs={{0,1},{1,0},{2,3},{3,2},{4,5},{5,4},{6,7},{7,6},{8,9},{9,8},{10,11... | collective-permute-start | bytes 301064 | tf_op jit(solution)/shard_map/ppermute | solution.py:200
  59.5 5.8 %collective-permute-start.15 = (bf16[8,6272]{1,0:T(8,128)(2,1)S(1)}, bf16[8,6272]{1,0:T(8,128)(2,1)S(1)}, u32[]{:S(2)}, u32[]{:S(2)}) collective-permute-start(bf16[8,6272]{1,0:T(8,128)(2,1)S(1)} %get-tuple-element.24.refs_0_), channel_id=1, source_target_pairs={{0,2},{1,3},{2,0},{3,1},{4,6},{5,7},{6,4},{7,5},{8,10},{9,11},{10,... | collective-permute-start | bytes 301064 | tf_op jit(solution)/shard_map/ppermute | solution.py:200
  60.1 6.3 %collective-permute-start.16 = (bf16[8,6272]{1,0:T(8,128)(2,1)S(1)}, bf16[8,6272]{1,0:T(8,128)(2,1)S(1)}, u32[]{:S(2)}, u32[]{:S(2)}) collective-permute-start(bf16[8,6272]{1,0:T(8,128)(2,1)S(1)} %get-tuple-element.24.refs_0_), channel_id=1, source_target_pairs={{0,3},{1,2},{2,1},{3,0},{4,7},{5,6},{6,5},{7,4},{8,11},{9,10},{10,... | collective-permute-start | bytes 301064 | tf_op jit(solution)/shard_map/ppermute | solution.py:200
  68.0 4.4 %collective-permute-start.17 = (bf16[8,1792]{1,0:T(8,128)(2,1)S(1)}, bf16[8,1792]{1,0:T(8,128)(2,1)S(1)}, u32[]{:S(2)}, u32[]{:S(2)}) collective-permute-start(bf16[8,1792]{1,0:T(8,128)(2,1)S(1)} %down.1), channel_id=1, source_target_pairs={{0,4},{4,0},{8,12},{12,8},{1,5},{5,1},{9,13},{13,9},{2,6},{6,2},{1... | collective-permute-start | bytes 86024 | tf_op jit(solution)/shard_map/ppermute | solution.py:200
  68.0 4.8 %collective-permute-start.18 = (bf16[8,1792]{1,0:T(8,128)(2,1)S(1)}, bf16[8,1792]{1,0:T(8,128)(2,1)S(1)}, u32[]{:S(2)}, u32[]{:S(2)}) collective-permute-start(bf16[8,1792]{1,0:T(8,128)(2,1)S(1)} %down.1), channel_id=1, source_target_pairs={{0,8},{4,12},{8,0},{12,4},{1,9},{5,13},{9,1},{13,5},{2,10},{6,14},... | collective-permute-start | bytes 86024 | tf_op jit(solution)/shard_map/ppermute | solution.py:200
  69.9 5.7 %collective-permute-start.19 = (bf16[8,1792]{1,0:T(8,128)(2,1)S(1)}, bf16[8,1792]{1,0:T(8,128)(2,1)S(1)}, u32[]{:S(2)}, u32[]{:S(2)}) collective-permute-start(bf16[8,1792]{1,0:T(8,128)(2,1)S(1)} %down.1), channel_id=1, source_target_pairs={{0,12},{4,8},{8,4},{12,0},{1,13},{5,9},{9,5},{13,1},{2,14},{6,10},... | collective-permute-start | bytes 86024 | tf_op jit(solution)/shard_map/ppermute | solution.py:200

commit v2 on v1

--- a/solution.py
+++ b/solution.py
@@ -220,52 +220,73 @@
     return pl.BlockSpec(memory_space=pltpu.VMEM)
 
 
-def locate_kernel(capacity, slots, place, lengths, rank_near, index_near, rank_far, index_far, page, count):
+def stage_kernel(capacity, heads, place, lengths, rank_hbm, index_hbm, store, out_proj, up_value, *refs):
+    found, pages, out_vmem, up_vmem, rank, index, table_sem, bulk_sem = refs
+    tables = [
+        pltpu.make_async_copy(rank_hbm, rank, table_sem.at[0]),
+        pltpu.make_async_copy(index_hbm, index, table_sem.at[1]),
+    ]
+    share = pl.ds((place[1] % 2) * heads, heads)
+    bulk = [
+        pltpu.make_async_copy(store, pages, bulk_sem.at[0]),
+        pltpu.make_async_copy(up_value.at[share], up_vmem, bulk_sem.at[1]),
+        pltpu.make_async_copy(out_proj, out_vmem, bulk_sem.at[2]),
+    ]
+    for copy in tables + bulk:
+        copy.start()
+    for copy in tables:
+        copy.wait()
     me, column = place[0], place[1]
-    ranks = lengths.shape[0]
+    ranks, slots = rank.shape
+    size = ranks * capacity
     for step in range(ranks):
-        rank = me ^ step
-        length = lengths[rank, 0]
-        for side, (table, index) in enumerate(((rank_near, index_near), (rank_far, index_far))):
-            first = (step * 2 + side) * capacity
-            for k in range(capacity):
-                page[first + k] = 0
-                count[first + k] = 0
-            base = (column ^ side) * slots
-
-            def visit(slot, found):
-                here = table[rank, slot] == me
-
-                @pl.when(here)
-                def _():
-                    page[first + found] = index[rank, slot]
-                    start = ((base + slot) % PAGES) * PAGE
-                    count[first + found] = jnp.clip(length - start, 0, PAGE)
-
-                return found + here.astype(jnp.int32)
-
-            lax.fori_loop(0, slots, visit, 0)
-
-
-def attend_kernel(capacity, heads, place, page, count, *refs):
-    ranks = (len(refs) - 4) // 2
+        other = me ^ step
+        length = lengths[other]
+        first = step * capacity
+        for k in range(capacity):
+            found[first + k] = 0
+            found[size + first + k] = 0
+        seen = jnp.int32(0)
+        for slot in range(slots):
+            here = rank[other, slot] == me
+
+            @pl.when(here)
+            def _():
+                start = ((column * slots + slot) % PAGES) * PAGE
+                found[first + seen] = index[other, slot]
+                found[size + first + seen] = jnp.clip(length - start, 0, PAGE)
+
+            seen = seen + here.astype(jnp.int32)
+    for copy in bulk:
+        copy.wait()
+
+
+def attend_kernel(capacity, heads, place, near_list, far_list, *refs):
+    ranks = (len(refs) - 5) // 2
     query_refs, (near, far, fresh) = refs[:ranks], refs[ranks : ranks + 3]
-    out_refs, held = refs[ranks + 3 : -1], refs[-1]
+    out_refs, (tall, held) = refs[ranks + 3 : -2], refs[-2:]
     me, column = place[0], place[1]
-    rows = query_refs[0].shape[0]
+    rows, latent = tall.shape
     steps = rows // (ranks * heads)
+    half = heads // 2
     lanes = lane_ids(rows)
     across = (((1,), (1,)), ((), ()))
     for step in range(ranks):
         rank = me ^ step
-        query = query_refs[step][...]
+        packed = query_refs[step][...].astype(jnp.float32)
+        for group in range(steps * ranks):
+            for odd in range(2):
+                tall[group * heads + odd * half : group * heads + (odd + 1) * half, :] = packed[
+                    group * half : (group + 1) * half, odd * latent : (odd + 1) * latent
+                ]
+        query = tall[...].astype(jnp.bfloat16)
         scores, values = [], []
-        for side, pages in enumerate((near, far)):
+        for pages, found in ((near, near_list), (far, far_list)):
             for k in range(capacity):
-                place_of = (step * 2 + side) * capacity + k
-                keys = pages.at[page[place_of]]
+                keys = pages.at[found[step * capacity + k]]
                 score = jnp.dot(query, keys[...], preferred_element_type=jnp.float32) * score_scale
-                scores.append(jnp.where(lanes < count[place_of], score, mask_value))
+                live = found[(ranks + step) * capacity + k]
+                scores.append(jnp.where(lanes < live, score, mask_value))
                 values.append(keys)
         peak = functools.reduce(jnp.maximum, scores)
         row_peak = jnp.max(peak, axis=1, keepdims=True)
@@ -309,11 +330,10 @@
             out[pl.ds(start, steps * heads), :] = jnp.concatenate(block, axis=0).astype(jnp.bfloat16)
 
 
-def lift_kernel(heads, ranks, place, *refs):
+def lift_kernel(heads, ranks, *refs):
     parts, up_value, out, joined, tall = refs[:ranks], refs[ranks], refs[ranks + 1], refs[-2], refs[-1]
     count = parts[0].shape[0]
     rows = count // heads
-    core = place[1] % 2
     blocks = [part[...].astype(jnp.float32) for part in parts]
     peaks = [b[:, CKV : CKV + 1] + b[:, CKV + 1 : CKV + 2] + b[:, CKV + 2 : CKV + 3] for b in blocks]
     totals = [b[:, CKV + 3 : CKV + 4] + b[:, CKV + 4 : CKV + 5] + b[:, CKV + 5 : CKV + 6] for b in blocks]
@@ -330,10 +350,10 @@
     lanes = lane_ids(rows)
     extra = jnp.zeros((rows, LANES), jnp.float32)
     for head in range(heads):
-        pick = pl.ds(head, rows, stride=heads)
+        pick = pl.ds(head % 2 * (heads // 2) + head // 2, rows, stride=heads)
         out[:, head * LANES : (head + 1) * LANES] = jnp.dot(
             jnp.concatenate([joined[g, pick, :] for g in range(CKV // LANES)], axis=1).astype(jnp.bfloat16),
-            up_value[core * heads + head],
+            up_value[head],
             preferred_element_type=jnp.float32,
         ).astype(jnp.bfloat16)
         extra = jnp.where(lanes % heads == head, tall[pick, :], extra)
@@ -345,10 +365,15 @@
 
 
 def project_kernel(heads, reps, place, *refs):
-    parts, (out_proj, own_rows, sent, kept) = refs[:reps], refs[reps:]
+    parts, (out_proj, residual, sent, kept) = refs[:reps], refs[reps:]
     core = place[1] % 2
     width = heads * LANES
-    result = own_rows[...]
+    rows, steps = kept.shape[0], residual.shape[0]
+    source = lax.broadcasted_iota(jnp.int32, (rows, steps), 0) - place[0] * steps
+    own = source == lax.broadcasted_iota(jnp.int32, (rows, steps), 1)
+    result = jnp.dot(
+        own.astype(jnp.bfloat16), residual[...], preferred_element_type=jnp.float32
+    )
     for side in range(2):
         blocks = [parts[step][...].astype(jnp.float32) for step in range(side, reps, 2)]
         tails = [b[:, width:] for b in blocks]
@@ -459,35 +484,47 @@
 
     share = lax.dynamic_index_in_dim(
         queries.reshape(steps, ranks, 2, heads * latent), column % 2, 2, keepdims=False
-    )
+    ).reshape(rows * heads // 2, 2 * latent)
     arrived = [share] + partners(share, "dp")
-    near = latent_store[0]
-    far = lax.ppermute(near, "rep", core_pairs)
-    tables = lax.ppermute(jnp.stack([page_rank, page_index]), "rep", core_pairs)
-    found = 2 * ranks * capacity
-    page, count = call(
-        functools.partial(locate_kernel, capacity, slots),
-        "locate",
-        (place, lengths, page_rank, page_index, tables[0], tables[1]),
-        [smem()] * 6,
-        [shape_of((found,), jnp.int32)] * 2,
-        4 * MIB,
-        out_specs=[smem()] * 2,
-    )
-    fresh = jnp.concatenate([new_latent, jnp.zeros((8 - steps, latent), new_latent.dtype)])
-    own_rows = jnp.where(
-        (jnp.arange(rows) // steps == me)[:, None], jnp.tile(residual.astype(jnp.float32), (ranks, 1)), 0.0
-    )
-    query_rows = [a.reshape(steps * ranks * heads, latent) for a in arrived]
+    store = latent_store[0]
+    far = lax.ppermute(store, "rep", core_pairs)
+    found, near, out_near, up_near = call(
+        functools.partial(stage_kernel, capacity, heads),
+        "stage",
+        (
+            place,
+            lengths.reshape(ranks),
+            *[pltpu.with_memory_space_constraint(a, pltpu.HBM) for a in (page_rank, page_index, store, out_proj, up_value)],
+        ),
+        [smem()] * 2 + [pl.BlockSpec(memory_space=pltpu.HBM)] * 5,
+        [
+            shape_of((2 * ranks * capacity,), jnp.int32),
+            pltpu.VMEM(store.shape, store.dtype),
+            pltpu.VMEM(out_proj.shape, out_proj.dtype),
+            pltpu.VMEM((heads, *up_value.shape[1:]), up_value.dtype),
+        ],
+        6 * MIB,
+        out_specs=[smem()] + [vmem()] * 3,
+        moved=2 * (store.size + out_proj.size),
+        scratch=[
+            pltpu.SMEM(page_rank.shape, jnp.int32),
+            pltpu.SMEM(page_rank.shape, jnp.int32),
+            pltpu.SemaphoreType.DMA((2,)),
+            pltpu.SemaphoreType.DMA((3,)),
+        ],
+    )
     width = CKV + LANES
     partial_rows = call(
         functools.partial(attend_kernel, capacity, heads),
         "attend",
-        (place, page, count, *query_rows, near, far, fresh),
+        (place, found, lax.ppermute(found, "rep", core_pairs), *arrived, near, far, new_latent),
         [smem()] * 3 + [vmem()] * (ranks + 3),
         [shape_of((rows * heads, width))] * ranks,
-        12 * MIB,
-        scratch=[pltpu.VMEM((steps * ranks * heads, width), jnp.float32)],
+        6 * MIB,
+        scratch=[
+            pltpu.VMEM((rows * heads, latent), jnp.float32),
+            pltpu.VMEM((rows * heads, width), jnp.float32),
+        ],
         flops=2 * 2 * slots * PAGE * rows * heads * latent,
         moved=2 * near.size * 2,
     )
@@ -497,24 +534,24 @@
     lifted = call(
         functools.partial(lift_kernel, heads, ranks),
         "lift",
-        (place, *joined, up_value),
-        [smem()] + [vmem()] * (ranks + 1),
+        (*joined, up_near),
+        [vmem()] * (ranks + 1),
         shape_of((rows, (heads + 1) * LANES)),
-        8 * MIB,
+        6 * MIB,
         scratch=[
             pltpu.VMEM((CKV // LANES, rows * heads, LANES), jnp.float32),
             pltpu.VMEM((rows * heads, LANES), jnp.float32),
         ],
         flops=2 * rows * heads * CKV * LANES,
-        moved=up_value.size * 2,
+        moved=up_near.size * 2,
     )
     sent, kept = call(
         functools.partial(project_kernel, heads, reps),
         "project",
-        (place, lifted, *partners(lifted, "rep"), out_proj, own_rows),
+        (place, lifted, *partners(lifted, "rep"), out_near, residual),
         [smem()] + [vmem()] * (reps + 2),
         [shape_of((rows, columns)), shape_of((rows, columns), jnp.float32)],
-        12 * MIB,
+        6 * MIB,
         flops=2 * rows * out_proj.size,
         moved=out_proj.size * 2,
     )
@@ -524,7 +561,7 @@
         (kept, *partners(sent, "dp"), norm_gain.reshape(1, columns), w_gate, w_up),
         [vmem()] * (ranks + 3),
         [shape_of((rows, 2 * w_gate.shape[1] + LANES)), shape_of((rows, columns), jnp.float32)],
-        28 * MIB,
+        6 * MIB,
         flops=4 * rows * w_gate.size,
         moved=w_gate.size * 4,
     )
@@ -534,7 +571,7 @@
         (gate_up, *partners(gate_up, "rep"), w_down),
         [vmem()] * (reps + 1),
         shape_of((rows, columns)),
-        16 * MIB,
+        6 * MIB,
         flops=2 * rows * w_down.size,
         moved=w_down.size * 2,
     )

time: 76.6 us -> 65.4 us (0.85)
  local copies, waits for them, and re-layouts: 15.8 us -> 2.24 us
  Pallas kernels: 13.2 us -> 15.4 us
  waiting for transfers between devices: 22.5 us -> 23.5 us
  other arithmetic: 1.49 us -> 0.71 us
    unnamed x21 -> x22, local copies, waits for them, and re-layouts: 12.6 us -> 0.7 us
    pallas_call x6, Pallas kernels: 13.2 us -> 15.4 us  [call(): pl.pallas_call(kernel, name=name, out_shape=outputs, in_specs=specs, out_...]
    ppermute x2, waiting for transfers between devices: 0.01 us -> 1.15 us  [the longest x1 1.15 us: queries_moved(): lax.ppermute(found, 'rep', core_pairs)]
  transfers between devices with their start and end apart: 20 -> 20, of which waited for: 10 -> 11; matrix products, arithmetic and copies ran while one was open for 6% -> 2% of each run, Pallas kernels for 4% -> 8%
where the time goes in v2:
time: 65.4 us; the launch traced here: 65.2 us
  waiting for transfers between devices  23.5 us (36%)
  starting transfers between devices  23.1 us (35%)
  Pallas kernels  15.4 us (24%)
  local copies, waits for them, and re-layouts  2.24 us (3%)
  other arithmetic  0.71 us (1%)
    ppermute x15, starting transfers between devices, partners(): lax.ppermute(array, axis, [(i, i ^ step) for i in range(size)])  18.1 us
    ppermute x15, waiting for transfers between devices, partners(): lax.ppermute(array, axis, [(i, i ^ step) for i in range(size)])  15.8 us
    pallas_call x6, Pallas kernels, call(): pl.pallas_call(kernel, name=name, out_shape=outputs, in_specs=specs, out_...  15.4 us
    ppermute x3, waiting for transfers between devices, queries_moved(): lax.ppermute(partial_rows[s], 'dp', [(i, i ^ s) for i in range(ranks)])  6.64 us
    ppermute x3, starting transfers between devices, queries_moved(): lax.ppermute(partial_rows[s], 'dp', [(i, i ^ s) for i in range(ranks)])  4.47 us
  transfers between devices with their start and end apart: 20, of which 11 were waited for; matrix products, arithmetic and copies ran while one was open for 2% of the time, Pallas kernels for 8%

profile of v2, /device:TPU:0, one launch (start us, length us, event | category | flops | bytes accessed | tf_op | source)
XLA Modules:
  0.0 65.2 jit_solution(7296715976103126548)
XLA Ops:
  0.0 0.5 collective-permute-start.4
  0.5 1.0 %reshape.14 = bf16[2,4,2,4608]{3,2,1,0:T(2,128)(2,1)S(1)} reshape(bf16[2,36864]{1,0:T(2,128)(2,1)} %param.17) | data formatting | bytes 294912 | tf_op jit(solution)/shard_map/reshape | solution.py:486
  1.5 0.0 copy-start.1
  1.5 0.5 dynamic-slice_reduce_fusion
  2.0 0.1 reshape.15.refs_0_
  2.1 2.6 %collective-permute-start.1 = (bf16[32,1152]{1,0:T(8,128)(2,1)S(1)}, bf16[32,1152]{1,0:T(8,128)(2,1)S(1)}, u32[]{:S(2)}, u32[]{:S(2)}) collective-permute-start(bf16[32,1152]{1,0:T(8,128)(2,1)S(1)} %reshape.15.refs_0_), channel_id=1, source_target_pairs={{0,4},{4,0},{8,12},{12,8},{1,5},{5,1},{9,13},{13,9},{2,6},{6,2},{1... | collective-permute-start | bytes 221192 | tf_op jit(solution)/shard_map/ppermute | solution.py:200
  4.7 2.6 %collective-permute-start.2 = (bf16[32,1152]{1,0:T(8,128)(2,1)S(1)}, bf16[32,1152]{1,0:T(8,128)(2,1)S(1)}, u32[]{:S(2)}, u32[]{:S(2)}) collective-permute-start(bf16[32,1152]{1,0:T(8,128)(2,1)S(1)} %reshape.15.refs_0_), channel_id=1, source_target_pairs={{0,8},{4,12},{8,0},{12,4},{1,9},{5,13},{9,1},{13,5},{2,10},{6,14},... | collective-permute-start | bytes 221192 | tf_op jit(solution)/shard_map/ppermute | solution.py:200
  7.3 0.0 collective-permute-start.3
  7.3 0.1 pad_add_fusion.place
  7.4 0.7 %copy-done.3 = s32[4,1]{0,1:T(1,128)S(1)} copy-done((s32[4,1]{0,1:T(1,128)S(1)}, s32[4,1]{0,1:T(1,128)}, u32[]{:S(2)}) %copy-start.3) | copy-done | bytes 40
  8.0 5.4 %stage.1 = (s32[24]{0:T(128)S(1)}, bf16[12,576,128]{2,1,0:T(8,128)(2,1)S(1)}, bf16[2048,1792]{1,0:T(8,128)(2,1)S(1)}, bf16[8,512,128]{2,1,0:T(8,128)(2,1)S(1)}) custom-call(s32[2]{0:T(128)S(1)} %pad_add_fusion.place, s32[4]{0:T(128)S(1)} %bitcast.8, s32[4,12]{1,0:T(4,128)} %rank_hbm.1, s32[4,12]{1,0:T(4,128)} %index_hbm.1, bf16[12,576,128]{2,1,0:T(8,128)(2,1)} %bitcast.10, ...), custom_call_target="tpu_custom_call" | custom-call | bytes 9109504 | tf_op jit(solution)/shard_map/stage/pallas_call | solution.py:442
  13.4 0.0 copy-start.4
  13.4 0.1 collective-permute-start
  13.5 1.1 %collective-permute-done.far_list = s32[24]{0:T(128)S(1)} collective-permute-done((s32[24]{0:T(128)S(1)}, s32[24]{0:T(128)S(1)}, u32[]{:S(2)}, u32[]{:S(2)}) %collective-permute-start) | collective-permute-done | bytes 128 | tf_op jit(solution)/shard_map/ppermute | solution.py:520
  14.7 0.0 collective-permute-done.1.refs_1_
  14.7 0.0 collective-permute-done.2.refs_2_
  14.7 0.0 collective-permute-done.3.refs_3_
  14.7 0.0 collective-permute-done.4.refs_5_
  14.7 0.0 copy-done.2
  14.7 3.3 %attend.1 = (bf16[64,640]{1,0:T(8,128)(2,1)S(1)}, bf16[64,640]{1,0:T(8,128)(2,1)S(1)}, bf16[64,640]{1,0:T(8,128)(2,1)S(1)}, bf16[64,640]{1,0:T(8,128)(2,1)S(1)}) custom-call(s32[2]{0:T(128)S(1)} %pad_add_fusion.place, s32[24]{0:T(128)S(1)} %get-tuple-element.17.near_list, s32[24]{0:T(128)S(1)} %collective-permute-done.far_list, ...), custom_call_target="tpu_custom_call" | custom-call | flops 226492416 | bytes 3538944 | tf_op jit(solution)/shard_map/attend/pallas_call | solution.py:442
  18.0 1.0 %collective-permute-start.5 = (bf16[64,640]{1,0:T(8,128)(2,1)S(1)}, bf16[64,640]{1,0:T(8,128)(2,1)S(1)}, u32[]{:S(2)}, u32[]{:S(2)}) collective-permute-start(bf16[64,640]{1,0:T(8,128)(2,1)S(1)} %get-tuple-element.20), channel_id=1, source_target_pairs={{0,4},{4,0},{8,12},{12,8},{1,5},{5,1},{9,13},{13,9},{2,6},{6,2},{1... | collective-permute-start | bytes 245768 | tf_op jit(solution)/shard_map/ppermute | solution.py:532
  18.9 3.5 %collective-permute-start.6 = (bf16[64,640]{1,0:T(8,128)(2,1)S(1)}, bf16[64,640]{1,0:T(8,128)(2,1)S(1)}, u32[]{:S(2)}, u32[]{:S(2)}) collective-permute-start(bf16[64,640]{1,0:T(8,128)(2,1)S(1)} %get-tuple-element.21), channel_id=1, source_target_pairs={{0,8},{4,12},{8,0},{12,4},{1,9},{5,13},{9,1},{13,5},{2,10},{6,14},... | collective-permute-start | bytes 245768 | tf_op jit(solution)/shard_map/ppermute | solution.py:532
  22.4 0.0 collective-permute-start.7
  22.5 0.1 collective-permute-done.5.refs_1_
  22.6 6.5 %collective-permute-done.6.refs_2_ = bf16[64,640]{1,0:T(8,128)(2,1)S(1)} collective-permute-done((bf16[64,640]{1,0:T(8,128)(2,1)S(1)}, bf16[64,640]{1,0:T(8,128)(2,1)S(1)}, u32[]{:S(2)}, u32[]{:S(2)}) %collective-permute-start.6) | collective-permute-done | bytes 81952 | tf_op jit(solution)/shard_map/ppermute | solution.py:532
  29.1 0.0 collective-permute-done.7.refs_3_
  29.1 0.5 lift.1.refs_0_
  29.6 0.1 collective-permute-start.10
  29.6 1.6 %collective-permute-start.8 = (bf16[8,1152]{1,0:T(8,128)(2,1)S(1)}, bf16[8,1152]{1,0:T(8,128)(2,1)S(1)}, u32[]{:S(2)}, u32[]{:S(2)}) collective-permute-start(bf16[8,1152]{1,0:T(8,128)(2,1)S(1)} %lift.1.refs_0_), channel_id=1, source_target_pairs={{0,1},{1,0},{2,3},{3,2},{4,5},{5,4},{6,7},{7,6},{8,9},{9,8},{10,11... | collective-permute-start | bytes 55304 | tf_op jit(solution)/shard_map/ppermute | solution.py:200
  31.2 0.5 collective-permute-start.9
  31.8 1.2 %collective-permute-done.10.refs_3_ = bf16[8,1152]{1,0:T(8,128)(2,1)S(1)} collective-permute-done((bf16[8,1152]{1,0:T(8,128)(2,1)S(1)}, bf16[8,1152]{1,0:T(8,128)(2,1)S(1)}, u32[]{:S(2)}, u32[]{:S(2)}) %collective-permute-start.10) | collective-permute-done | bytes 18464 | tf_op jit(solution)/shard_map/ppermute | solution.py:200
  33.0 0.0 collective-permute-done.8.refs_1_
  33.0 2.0 %collective-permute-done.9.refs_2_ = bf16[8,1152]{1,0:T(8,128)(2,1)S(1)} collective-permute-done((bf16[8,1152]{1,0:T(8,128)(2,1)S(1)}, bf16[8,1152]{1,0:T(8,128)(2,1)S(1)}, u32[]{:S(2)}, u32[]{:S(2)}) %collective-permute-start.9) | collective-permute-done | bytes 18464 | tf_op jit(solution)/shard_map/ppermute | solution.py:200
  35.0 0.0 copy-done.1
  35.0 1.8 %project.1 = (bf16[8,1792]{1,0:T(8,128)(2,1)S(1)}, f32[8,1792]{1,0:T(8,128)S(1)}) custom-call(s32[2]{0:T(128)S(1)} %pad_add_fusion.place, bf16[8,1152]{1,0:T(8,128)(2,1)S(1)} %lift.1.refs_0_, bf16[8,1152]{1,0:T(8,128)(2,1)S(1)} %collective-permute-done.8.refs_1_, bf16[8,1152]{1,0:T(8,128)(2,1)S(1)} %collective-permute-done.9.refs_2_, ...), custom_call_target="tpu_custom_call" | custom-call | flops 58720256 | bytes 7340032 | tf_op jit(solution)/shard_map/project/pallas_call | solution.py:442
  36.7 1.7 %collective-permute-start.11 = (bf16[8,1792]{1,0:T(8,128)(2,1)S(1)}, bf16[8,1792]{1,0:T(8,128)(2,1)S(1)}, u32[]{:S(2)}, u32[]{:S(2)}) collective-permute-start(bf16[8,1792]{1,0:T(8,128)(2,1)S(1)} %get-tuple-element.26), channel_id=1, source_target_pairs={{0,4},{4,0},{8,12},{12,8},{1,5},{5,1},{9,13},{13,9},{2,6},{6,2},{1... | collective-permute-start | bytes 86024 | tf_op jit(solution)/shard_map/ppermute | solution.py:200
  38.4 1.5 %collective-permute-start.12 = (bf16[8,1792]{1,0:T(8,128)(2,1)S(1)}, bf16[8,1792]{1,0:T(8,128)(2,1)S(1)}, u32[]{:S(2)}, u32[]{:S(2)}) collective-permute-start(bf16[8,1792]{1,0:T(8,128)(2,1)S(1)} %get-tuple-element.26), channel_id=1, source_target_pairs={{0,8},{4,12},{8,0},{12,4},{1,9},{5,13},{9,1},{13,5},{2,10},{6,14},... | collective-permute-start | bytes 86024 | tf_op jit(solution)/shard_map/ppermute | solution.py:200
  39.9 1.2 %collective-permute-start.13 = (bf16[8,1792]{1,0:T(8,128)(2,1)S(1)}, bf16[8,1792]{1,0:T(8,128)(2,1)S(1)}, u32[]{:S(2)}, u32[]{:S(2)}) collective-permute-start(bf16[8,1792]{1,0:T(8,128)(2,1)S(1)} %get-tuple-element.26), channel_id=1, source_target_pairs={{0,12},{4,8},{8,4},{12,0},{1,13},{5,9},{9,5},{13,1},{2,14},{6,10},... | collective-permute-start | bytes 86024 | tf_op jit(solution)/shard_map/ppermute | solution.py:200
  41.1 0.0 copy-done.4
  41.2 0.0 collective-permute-done.11.refs_1_
  41.2 2.5 %collective-permute-done.12.refs_2_ = bf16[8,1792]{1,0:T(8,128)(2,1)S(1)} collective-permute-done((bf16[8,1792]{1,0:T(8,128)(2,1)S(1)}, bf16[8,1792]{1,0:T(8,128)(2,1)S(1)}, u32[]{:S(2)}, u32[]{:S(2)}) %collective-permute-start.12) | collective-permute-done | bytes 28704 | tf_op jit(solution)/shard_map/ppermute | solution.py:200
  43.7 2.0 %collective-permute-done.13.refs_3_ = bf16[8,1792]{1,0:T(8,128)(2,1)S(1)} collective-permute-done((bf16[8,1792]{1,0:T(8,128)(2,1)S(1)}, bf16[8,1792]{1,0:T(8,128)(2,1)S(1)}, u32[]{:S(2)}, u32[]{:S(2)}) %collective-permute-start.13) | collective-permute-done | bytes 28704 | tf_op jit(solution)/shard_map/ppermute | solution.py:200
  45.6 0.0 slice-done
  45.6 0.0 slice-done.1
  45.6 0.0 copy-done
  45.6 0.0 slice-done.2
  45.6 0.0 slice-start.4
  45.7 0.0 slice-start.5
  45.7 3.0 %gate.1 = (bf16[8,6272]{1,0:T(8,128)(2,1)S(1)}, f32[8,1792]{1,0:T(8,128)S(1)}) custom-call(f32[8,1792]{1,0:T(8,128)S(1)} %get-tuple-element.25.refs_0_, bf16[8,1792]{1,0:T(8,128)(2,1)S(1)} %collective-permute-done.11.refs_1_, bf16[8,1792]{1,0:T(8,128)(2,1)S(1)} %collective-permute-done.12.refs_2_, bf16[8,1792]{1,0:T(8,128)(2,1)S(1)} %collective-permute-done.13.refs_3_, ...), custom_call_target="tpu_custom_call" | custom-call | flops 176160768 | bytes 22020096 | tf_op jit(solution)/shard_map/gate/pallas_call | solution.py:442
  48.6 0.0 collective-permute-start.14
  48.6 0.6 collective-permute-start.15
  49.2 1.3 %collective-permute-start.16 = (bf16[8,6272]{1,0:T(8,128)(2,1)S(1)}, bf16[8,6272]{1,0:T(8,128)(2,1)S(1)}, u32[]{:S(2)}, u32[]{:S(2)}) collective-permute-start(bf16[8,6272]{1,0:T(8,128)(2,1)S(1)} %get-tuple-element.28.refs_0_), channel_id=1, source_target_pairs={{0,3},{1,2},{2,1},{3,0},{4,7},{5,6},{6,5},{7,4},{8,11},{9,10},{10,... | collective-permute-start | bytes 301064 | tf_op jit(solution)/shard_map/ppermute | solution.py:200
  50.5 0.0 collective-permute-done.14.refs_1_
  50.5 3.9 %collective-permute-done.15.refs_2_ = bf16[8,6272]{1,0:T(8,128)(2,1)S(1)} collective-permute-done((bf16[8,6272]{1,0:T(8,128)(2,1)S(1)}, bf16[8,6272]{1,0:T(8,128)(2,1)S(1)}, u32[]{:S(2)}, u32[]{:S(2)}) %collective-permute-start.15) | collective-permute-done | bytes 100384 | tf_op jit(solution)/shard_map/ppermute | solution.py:200
  54.4 1.1 %collective-permute-done.16.refs_3_ = bf16[8,6272]{1,0:T(8,128)(2,1)S(1)} collective-permute-done((bf16[8,6272]{1,0:T(8,128)(2,1)S(1)}, bf16[8,6272]{1,0:T(8,128)(2,1)S(1)}, u32[]{:S(2)}, u32[]{:S(2)}) %collective-permute-start.16) | collective-permute-done | bytes 100384 | tf_op jit(solution)/shard_map/ppermute | solution.py:200
  55.5 0.0 slice-done.3
  55.6 1.6 %down.1 = bf16[8,1792]{1,0:T(8,128)(2,1)S(1)} custom-call(bf16[8,6272]{1,0:T(8,128)(2,1)S(1)} %get-tuple-element.28.refs_0_, bf16[8,6272]{1,0:T(8,128)(2,1)S(1)} %collective-permute-done.14.refs_1_, bf16[8,6272]{1,0:T(8,128)(2,1)S(1)} %collective-permute-done.15.refs_2_, bf16[8,6272]{1,0:T(8,128)(2,1)S(1)} %collective-permute-done.16.refs_3_, ...), custom_call_target="tpu_custom_call" | custom-call | flops 88080384 | bytes 11010048 | tf_op jit(solution)/shard_map/down/pallas_call | solution.py:442
  57.2 0.0 collective-permute-start.17
  57.2 1.8 %collective-permute-start.18 = (bf16[8,1792]{1,0:T(8,128)(2,1)S(1)}, bf16[8,1792]{1,0:T(8,128)(2,1)S(1)}, u32[]{:S(2)}, u32[]{:S(2)}) collective-permute-start(bf16[8,1792]{1,0:T(8,128)(2,1)S(1)} %down.1), channel_id=1, source_target_pairs={{0,8},{4,12},{8,0},{12,4},{1,9},{5,13},{9,1},{13,5},{2,10},{6,14},... | collective-permute-start | bytes 86024 | tf_op jit(solution)/shard_map/ppermute | solution.py:200
  58.9 2.6 %collective-permute-start.19 = (bf16[8,1792]{1,0:T(8,128)(2,1)S(1)}, bf16[8,1792]{1,0:T(8,128)(2,1)S(1)}, u32[]{:S(2)}, u32[]{:S(2)}) collective-permute-start(bf16[8,1792]{1,0:T(8,128)(2,1)S(1)} %down.1), channel_id=1, source_target_pairs={{0,12},{4,8},{8,4},{12,0},{1,13},{5,9},{9,5},{13,1},{2,14},{6,10},... | collective-permute-start | bytes 86024 | tf_op jit(solution)/shard_map/ppermute | solution.py:200
  61.5 0.0 collective-permute-done.17
  61.6 0.4 collective-permute-done.18
  62.0 2.6 %collective-permute-done.19 = bf16[8,1792]{1,0:T(8,128)(2,1)S(1)} collective-permute-done((bf16[8,1792]{1,0:T(8,128)(2,1)S(1)}, bf16[8,1792]{1,0:T(8,128)(2,1)S(1)}, u32[]{:S(2)}, u32[]{:S(2)}) %collective-permute-start.19) | collective-permute-done | bytes 28704 | tf_op jit(solution)/shard_map/ppermute | solution.py:200
  64.6 0.6 add_convert_fusion
  (12 shorter events, 0.0 us)
Async XLA Ops:
  0.0 14.7 %copy-start.2 = (bf16[2,576]{1,0:T(2,128)(2,1)S(1)}, bf16[2,576]{1,0:T(2,128)(2,1)}, u32[]{:S(2)}) copy-start(bf16[2,576]{1,0:T(2,128)(2,1)} %refs_6_.2) | copy-start | bytes 6916
  0.0 14.7 %collective-permute-start.4 = (bf16[12,576,128]{2,1,0:T(8,128)(2,1)}, bf16[12,576,128]{2,1,0:T(8,128)(2,1)S(1)}, u32[]{:S(2)}, u32[]{:S(2)}) collective-permute-start(bf16[12,576,128]{2,1,0:T(8,128)(2,1)} %bitcast.9), channel_id=1, source_target_pairs={{0,1},{1,0},{2,3},{3,2},{4,5},{5,4},{6,7},{7,6},{8,9},{9,8},{10,11... | collective-permute-start | bytes 5308424 | tf_op jit(solution)/shard_map/ppermute | solution.py:490
  1.5 33.5 %copy-start.1 = (bf16[2,1792]{1,0:T(2,128)(2,1)S(1)}, bf16[2,1792]{1,0:T(2,128)(2,1)}, u32[]{:S(2)}) copy-start(bf16[2,1792]{1,0:T(2,128)(2,1)} %refs_5_.2) | copy-start | bytes 21508
  2.1 12.6 %collective-permute-start.1 = (bf16[32,1152]{1,0:T(8,128)(2,1)S(1)}, bf16[32,1152]{1,0:T(8,128)(2,1)S(1)}, u32[]{:S(2)}, u32[]{:S(2)}) collective-permute-start(bf16[32,1152]{1,0:T(8,128)(2,1)S(1)} %reshape.15.refs_0_), channel_id=1, source_target_pairs={{0,4},{4,0},{8,12},{12,8},{1,5},{5,1},{9,13},{13,9},{2,6},{6,2},{1... | collective-permute-start | bytes 221192 | tf_op jit(solution)/shard_map/ppermute | solution.py:200
  4.7 10.0 %collective-permute-start.2 = (bf16[32,1152]{1,0:T(8,128)(2,1)S(1)}, bf16[32,1152]{1,0:T(8,128)(2,1)S(1)}, u32[]{:S(2)}, u32[]{:S(2)}) collective-permute-start(bf16[32,1152]{1,0:T(8,128)(2,1)S(1)} %reshape.15.refs_0_), channel_id=1, source_target_pairs={{0,8},{4,12},{8,0},{12,4},{1,9},{5,13},{9,1},{13,5},{2,10},{6,14},... | collective-permute-start | bytes 221192 | tf_op jit(solution)/shard_map/ppermute | solution.py:200
  7.3 7.4 %collective-permute-start.3 = (bf16[32,1152]{1,0:T(8,128)(2,1)S(1)}, bf16[32,1152]{1,0:T(8,128)(2,1)S(1)}, u32[]{:S(2)}, u32[]{:S(2)}) collective-permute-start(bf16[32,1152]{1,0:T(8,128)(2,1)S(1)} %reshape.15.refs_0_), channel_id=1, source_target_pairs={{0,12},{4,8},{8,4},{12,0},{1,13},{5,9},{9,5},{13,1},{2,14},{6,10},... | collective-permute-start | bytes 221192 | tf_op jit(solution)/shard_map/ppermute | solution.py:200
  7.4 0.7 %copy-start.3 = (s32[4,1]{0,1:T(1,128)S(1)}, s32[4,1]{0,1:T(1,128)}, u32[]{:S(2)}) copy-start(s32[4,1]{0,1:T(1,128)} %param.16) | copy-start | bytes 52
  8.0 37.6 %slice-start = ((s8[11010048]{0:T(1024)(128)(4,1)}), s8[4194304]{0:T(1024)(128)(4,1)S(1)}, s32[]{:S(2)}) async-start(s8[11010048]{0:T(1024)(128)(4,1)} %bitcast.4), calls=%async_computation | async-start | bytes 8388608
  8.0 37.6 %slice-start.1 = ((s8[11010048]{0:T(1024)(128)(4,1)}), s8[4194304]{0:T(1024)(128)(4,1)S(1)}, s32[]{:S(2)}) async-start(s8[11010048]{0:T(1024)(128)(4,1)} %bitcast.4), calls=%async_computation.1 | async-start | bytes 8388608
  8.0 37.6 %copy-start = (bf16[1792,3072]{1,0:T(8,128)(2,1)S(1)}, bf16[1792,3072]{1,0:T(8,128)(2,1)}, u32[]{:S(2)}) copy-start(bf16[1792,3072]{1,0:T(8,128)(2,1)} %refs_6_.3) | copy-start | bytes 33030148
  13.4 27.7 %copy-start.4 = (f32[1792]{0:T(1024)S(1)}, f32[1792]{0:T(1024)}, u32[]{:S(2)}) copy-start(f32[1792]{0:T(1024)} %param.22) | copy-start | bytes 21508
  13.4 1.2 %collective-permute-start = (s32[24]{0:T(128)S(1)}, s32[24]{0:T(128)S(1)}, u32[]{:S(2)}, u32[]{:S(2)}) collective-permute-start(s32[24]{0:T(128)S(1)} %get-tuple-element.17.near_list), channel_id=1, source_target_pairs={{0,1},{1,0},{2,3},{3,2},{4,5},{5,4},{6,7},{7,6},{8,9},{9,8},{10,11... | collective-permute-start | bytes 296 | tf_op jit(solution)/shard_map/ppermute | solution.py:520
  18.0 4.6 %collective-permute-start.5 = (bf16[64,640]{1,0:T(8,128)(2,1)S(1)}, bf16[64,640]{1,0:T(8,128)(2,1)S(1)}, u32[]{:S(2)}, u32[]{:S(2)}) collective-permute-start(bf16[64,640]{1,0:T(8,128)(2,1)S(1)} %get-tuple-element.20), channel_id=1, source_target_pairs={{0,4},{4,0},{8,12},{12,8},{1,5},{5,1},{9,13},{13,9},{2,6},{6,2},{1... | collective-permute-start | bytes 245768 | tf_op jit(solution)/shard_map/ppermute | solution.py:532
  18.9 10.2 %collective-permute-start.6 = (bf16[64,640]{1,0:T(8,128)(2,1)S(1)}, bf16[64,640]{1,0:T(8,128)(2,1)S(1)}, u32[]{:S(2)}, u32[]{:S(2)}) collective-permute-start(bf16[64,640]{1,0:T(8,128)(2,1)S(1)} %get-tuple-element.21), channel_id=1, source_target_pairs={{0,8},{4,12},{8,0},{12,4},{1,9},{5,13},{9,1},{13,5},{2,10},{6,14},... | collective-permute-start | bytes 245768 | tf_op jit(solution)/shard_map/ppermute | solution.py:532
  22.4 6.6 %collective-permute-start.7 = (bf16[64,640]{1,0:T(8,128)(2,1)S(1)}, bf16[64,640]{1,0:T(8,128)(2,1)S(1)}, u32[]{:S(2)}, u32[]{:S(2)}) collective-permute-start(bf16[64,640]{1,0:T(8,128)(2,1)S(1)} %get-tuple-element.22), channel_id=1, source_target_pairs={{0,12},{4,8},{8,4},{12,0},{1,13},{5,9},{9,5},{13,1},{2,14},{6,10},... | collective-permute-start | bytes 245768 | tf_op jit(solution)/shard_map/ppermute | solution.py:532
  29.1 16.5 %slice-start.2 = ((s8[11010048]{0:T(1024)(128)(4,1)}), s8[2621440]{0:T(1024)(128)(4,1)S(1)}, s32[]{:S(2)}) async-start(s8[11010048]{0:T(1024)(128)(4,1)} %bitcast.4), calls=%async_computation.2 | async-start | bytes 5242880
  29.6 3.4 %collective-permute-start.10 = (bf16[8,1152]{1,0:T(8,128)(2,1)S(1)}, bf16[8,1152]{1,0:T(8,128)(2,1)S(1)}, u32[]{:S(2)}, u32[]{:S(2)}) collective-permute-start(bf16[8,1152]{1,0:T(8,128)(2,1)S(1)} %lift.1.refs_0_), channel_id=1, source_target_pairs={{0,3},{1,2},{2,1},{3,0},{4,7},{5,6},{6,5},{7,4},{8,11},{9,10},{10,... | collective-permute-start | bytes 55304 | tf_op jit(solution)/shard_map/ppermute | solution.py:200
  29.6 3.3 %collective-permute-start.8 = (bf16[8,1152]{1,0:T(8,128)(2,1)S(1)}, bf16[8,1152]{1,0:T(8,128)(2,1)S(1)}, u32[]{:S(2)}, u32[]{:S(2)}) collective-permute-start(bf16[8,1152]{1,0:T(8,128)(2,1)S(1)} %lift.1.refs_0_), channel_id=1, source_target_pairs={{0,1},{1,0},{2,3},{3,2},{4,5},{5,4},{6,7},{7,6},{8,9},{9,8},{10,11... | collective-permute-start | bytes 55304 | tf_op jit(solution)/shard_map/ppermute | solution.py:200
  31.2 3.8 %collective-permute-start.9 = (bf16[8,1152]{1,0:T(8,128)(2,1)S(1)}, bf16[8,1152]{1,0:T(8,128)(2,1)S(1)}, u32[]{:S(2)}, u32[]{:S(2)}) collective-permute-start(bf16[8,1152]{1,0:T(8,128)(2,1)S(1)} %lift.1.refs_0_), channel_id=1, source_target_pairs={{0,2},{1,3},{2,0},{3,1},{4,6},{5,7},{6,4},{7,5},{8,10},{9,11},{10,... | collective-permute-start | bytes 55304 | tf_op jit(solution)/shard_map/ppermute | solution.py:200
  36.7 4.4 %collective-permute-start.11 = (bf16[8,1792]{1,0:T(8,128)(2,1)S(1)}, bf16[8,1792]{1,0:T(8,128)(2,1)S(1)}, u32[]{:S(2)}, u32[]{:S(2)}) collective-permute-start(bf16[8,1792]{1,0:T(8,128)(2,1)S(1)} %get-tuple-element.26), channel_id=1, source_target_pairs={{0,4},{4,0},{8,12},{12,8},{1,5},{5,1},{9,13},{13,9},{2,6},{6,2},{1... | collective-permute-start | bytes 86024 | tf_op jit(solution)/shard_map/ppermute | solution.py:200
  38.4 5.2 %collective-permute-start.12 = (bf16[8,1792]{1,0:T(8,128)(2,1)S(1)}, bf16[8,1792]{1,0:T(8,128)(2,1)S(1)}, u32[]{:S(2)}, u32[]{:S(2)}) collective-permute-start(bf16[8,1792]{1,0:T(8,128)(2,1)S(1)} %get-tuple-element.26), channel_id=1, source_target_pairs={{0,8},{4,12},{8,0},{12,4},{1,9},{5,13},{9,1},{13,5},{2,10},{6,14},... | collective-permute-start | bytes 86024 | tf_op jit(solution)/shard_map/ppermute | solution.py:200
  39.9 5.7 %collective-permute-start.13 = (bf16[8,1792]{1,0:T(8,128)(2,1)S(1)}, bf16[8,1792]{1,0:T(8,128)(2,1)S(1)}, u32[]{:S(2)}, u32[]{:S(2)}) collective-permute-start(bf16[8,1792]{1,0:T(8,128)(2,1)S(1)} %get-tuple-element.26), channel_id=1, source_target_pairs={{0,12},{4,8},{8,4},{12,0},{1,13},{5,9},{9,5},{13,1},{2,14},{6,10},... | collective-permute-start | bytes 86024 | tf_op jit(solution)/shard_map/ppermute | solution.py:200
  45.6 9.9 %slice-start.3 = ((s8[11010048]{0:T(1024)(128)(4,1)}), s8[4194304]{0:T(1024)(128)(4,1)S(1)}, s32[]{:S(2)}) async-start(s8[11010048]{0:T(1024)(128)(4,1)} %bitcast.6), calls=%async_computation.3 | async-start | bytes 8388608
  45.6 9.9 %slice-start.4 = ((s8[11010048]{0:T(1024)(128)(4,1)}), s8[4194304]{0:T(1024)(128)(4,1)S(1)}, s32[]{:S(2)}) async-start(s8[11010048]{0:T(1024)(128)(4,1)} %bitcast.6), calls=%async_computation.4 | async-start | bytes 8388608
  45.7 9.9 %slice-start.5 = ((s8[11010048]{0:T(1024)(128)(4,1)}), s8[2621440]{0:T(1024)(128)(4,1)S(1)}, s32[]{:S(2)}) async-start(s8[11010048]{0:T(1024)(128)(4,1)} %bitcast.6), calls=%async_computation.5 | async-start | bytes 5242880
  48.6 1.9 %collective-permute-start.14 = (bf16[8,6272]{1,0:T(8,128)(2,1)S(1)}, bf16[8,6272]{1,0:T(8,128)(2,1)S(1)}, u32[]{:S(2)}, u32[]{:S(2)}) collective-permute-start(bf16[8,6272]{1,0:T(8,128)(2,1)S(1)} %get-tuple-element.28.refs_0_), channel_id=1, source_target_pairs={{0,1},{1,0},{2,3},{3,2},{4,5},{5,4},{6,7},{7,6},{8,9},{9,8},{10,11... | collective-permute-start | bytes 301064 | tf_op jit(solution)/shard_map/ppermute | solution.py:200
  48.6 5.8 %collective-permute-start.15 = (bf16[8,6272]{1,0:T(8,128)(2,1)S(1)}, bf16[8,6272]{1,0:T(8,128)(2,1)S(1)}, u32[]{:S(2)}, u32[]{:S(2)}) collective-permute-start(bf16[8,6272]{1,0:T(8,128)(2,1)S(1)} %get-tuple-element.28.refs_0_), channel_id=1, source_target_pairs={{0,2},{1,3},{2,0},{3,1},{4,6},{5,7},{6,4},{7,5},{8,10},{9,11},{10,... | collective-permute-start | bytes 301064 | tf_op jit(solution)/shard_map/ppermute | solution.py:200
  49.2 6.3 %collective-permute-start.16 = (bf16[8,6272]{1,0:T(8,128)(2,1)S(1)}, bf16[8,6272]{1,0:T(8,128)(2,1)S(1)}, u32[]{:S(2)}, u32[]{:S(2)}) collective-permute-start(bf16[8,6272]{1,0:T(8,128)(2,1)S(1)} %get-tuple-element.28.refs_0_), channel_id=1, source_target_pairs={{0,3},{1,2},{2,1},{3,0},{4,7},{5,6},{6,5},{7,4},{8,11},{9,10},{10,... | collective-permute-start | bytes 301064 | tf_op jit(solution)/shard_map/ppermute | solution.py:200
  57.2 4.4 %collective-permute-start.17 = (bf16[8,1792]{1,0:T(8,128)(2,1)S(1)}, bf16[8,1792]{1,0:T(8,128)(2,1)S(1)}, u32[]{:S(2)}, u32[]{:S(2)}) collective-permute-start(bf16[8,1792]{1,0:T(8,128)(2,1)S(1)} %down.1), channel_id=1, source_target_pairs={{0,4},{4,0},{8,12},{12,8},{1,5},{5,1},{9,13},{13,9},{2,6},{6,2},{1... | collective-permute-start | bytes 86024 | tf_op jit(solution)/shard_map/ppermute | solution.py:200
  57.2 4.8 %collective-permute-start.18 = (bf16[8,1792]{1,0:T(8,128)(2,1)S(1)}, bf16[8,1792]{1,0:T(8,128)(2,1)S(1)}, u32[]{:S(2)}, u32[]{:S(2)}) collective-permute-start(bf16[8,1792]{1,0:T(8,128)(2,1)S(1)} %down.1), channel_id=1, source_target_pairs={{0,8},{4,12},{8,0},{12,4},{1,9},{5,13},{9,1},{13,5},{2,10},{6,14},... | collective-permute-start | bytes 86024 | tf_op jit(solution)/shard_map/ppermute | solution.py:200
  58.9 5.7 %collective-permute-start.19 = (bf16[8,1792]{1,0:T(8,128)(2,1)S(1)}, bf16[8,1792]{1,0:T(8,128)(2,1)S(1)}, u32[]{:S(2)}, u32[]{:S(2)}) collective-permute-start(bf16[8,1792]{1,0:T(8,128)(2,1)S(1)} %down.1), channel_id=1, source_target_pairs={{0,12},{4,8},{8,4},{12,0},{1,13},{5,9},{9,5},{13,1},{2,14},{6,10},... | collective-permute-start | bytes 86024 | tf_op jit(solution)/shard_map/ppermute | solution.py:200

commit v3 on v2

--- a/solution.py
+++ b/solution.py
@@ -7,6 +7,7 @@
 from jax.experimental import pallas as pl
 from jax.experimental.pallas import tpu as pltpu
 from jax.sharding import PartitionSpec as P
+
 
 CKV = 512
 PAGE = 128
@@ -194,11 +195,21 @@
     return (mixed_rows + mlp_out).astype(jnp.bfloat16)
 
 
-def partners(array, axis):
+def hops(size, name):
+    order = list(range(1, size))
+    if name in ("query", "partial"):
+        return [order[0], *reversed(order[1:])]
+    if name == "units":
+        return [order[-1], *order[:-1]]
+    return order
+
+
+def partners(arrays, axis, name):
     size = lax.axis_size(axis)
-    return [
-        lax.ppermute(array, axis, [(i, i ^ step) for i in range(size)]) for step in range(1, size)
-    ]
+    moved = {}
+    for step in hops(size, name):
+        moved[step] = lax.ppermute(arrays[step], axis, [(i, i ^ step) for i in range(size)])
+    return [moved[step] for step in range(1, size)]
 
 
 def thirds(value):
@@ -220,23 +231,51 @@
     return pl.BlockSpec(memory_space=pltpu.VMEM)
 
 
-def stage_kernel(capacity, heads, place, lengths, rank_hbm, index_hbm, store, out_proj, up_value, *refs):
-    found, pages, out_vmem, up_vmem, rank, index, table_sem, bulk_sem = refs
+def position():
+    return lax.axis_index("dp"), lax.axis_index("rep")
+
+
+def pack_kernel(queries, out, held, rows, sem):
+    _, column = position()
+    ranks, steps, width = held.shape
+    pairs = rows.shape[0] // (ranks * steps)
+    double = rows.shape[1]
+    copies = []
+    for rank in range(ranks):
+        start = pl.multiple_of((2 * rank + column % 2) * width, LANES)
+        copies.append(
+            pltpu.make_async_copy(queries.at[:, pl.ds(start, width)], held.at[rank], sem.at[rank])
+        )
+        copies[-1].start()
+    for rank, copy in enumerate(copies):
+        copy.wait()
+        part = held[rank].astype(jnp.float32)
+        for step in range(steps):
+            for pair in range(pairs):
+                row = (rank * steps + step) * pairs + pair
+                rows[row : row + 1, :] = part[step : step + 1, pair * double : (pair + 1) * double]
+    out[...] = rows[...].astype(jnp.bfloat16)
+
+
+def stage_kernel(capacity, heads, lengths_hbm, rank_hbm, index_hbm, store, up_value, new_latent, *refs):
+    found, pages, up_vmem, fresh, lengths, rank, index, table_sem, bulk_sem = refs
+    me, column = position()
     tables = [
-        pltpu.make_async_copy(rank_hbm, rank, table_sem.at[0]),
-        pltpu.make_async_copy(index_hbm, index, table_sem.at[1]),
+        pltpu.make_async_copy(source, target, table_sem.at[k])
+        for k, (source, target) in enumerate(
+            ((lengths_hbm, lengths), (rank_hbm, rank), (index_hbm, index))
+        )
     ]
-    share = pl.ds((place[1] % 2) * heads, heads)
+    share = pl.ds((column % 2) * heads, heads)
     bulk = [
         pltpu.make_async_copy(store, pages, bulk_sem.at[0]),
         pltpu.make_async_copy(up_value.at[share], up_vmem, bulk_sem.at[1]),
-        pltpu.make_async_copy(out_proj, out_vmem, bulk_sem.at[2]),
+        pltpu.make_async_copy(new_latent, fresh, bulk_sem.at[2]),
     ]
     for copy in tables + bulk:
         copy.start()
     for copy in tables:
         copy.wait()
-    me, column = place[0], place[1]
     ranks, slots = rank.shape
     size = ranks * capacity
     for step in range(ranks):
@@ -261,51 +300,48 @@
         copy.wait()
 
 
-def attend_kernel(capacity, heads, place, near_list, far_list, *refs):
-    ranks = (len(refs) - 5) // 2
-    query_refs, (near, far, fresh) = refs[:ranks], refs[ranks : ranks + 3]
-    out_refs, (tall, held) = refs[ranks + 3 : -2], refs[-2:]
-    me, column = place[0], place[1]
-    rows, latent = tall.shape
+def attend_kernel(capacity, heads, near_list, far_list, *refs):
+    ranks = (len(refs) - 7) // 2
+    query_refs, (near, far, fresh, out_proj) = refs[:ranks], refs[ranks : ranks + 4]
+    out_refs, (out_near, held, sem) = refs[ranks + 4 : -3], refs[-3:]
+    fetch = pltpu.make_async_copy(out_proj, out_near, sem)
+    fetch.start()
+    me, column = position()
+    rows = held.shape[1]
+    latent = fresh.shape[1]
     steps = rows // (ranks * heads)
     half = heads // 2
     lanes = lane_ids(rows)
     across = (((1,), (1,)), ((), ()))
     for step in range(ranks):
-        rank = me ^ step
-        packed = query_refs[step][...].astype(jnp.float32)
-        for group in range(steps * ranks):
-            for odd in range(2):
-                tall[group * heads + odd * half : group * heads + (odd + 1) * half, :] = packed[
-                    group * half : (group + 1) * half, odd * latent : (odd + 1) * latent
-                ]
-        query = tall[...].astype(jnp.bfloat16)
-        scores, values = [], []
-        for pages, found in ((near, near_list), (far, far_list)):
-            for k in range(capacity):
-                keys = pages.at[found[step * capacity + k]]
-                score = jnp.dot(query, keys[...], preferred_element_type=jnp.float32) * score_scale
-                live = found[(ranks + step) * capacity + k]
-                scores.append(jnp.where(lanes < live, score, mask_value))
-                values.append(keys)
-        peak = functools.reduce(jnp.maximum, scores)
-        row_peak = jnp.max(peak, axis=1, keepdims=True)
+        packed = query_refs[step][...]
+        query = jnp.concatenate([packed[:, 0:latent], packed[:, latent:]], axis=0)
+        scores, keys = [], []
+        for k in range(capacity):
+            pages, live = [], []
+            for side, table in ((near, near_list), (far, far_list)):
+                pages.append(side[table[step * capacity + k]])
+                live.append(lanes < table[(ranks + step) * capacity + k])
+            keys.append(jnp.concatenate(pages, axis=1))
+            score = jnp.dot(query, keys[-1], preferred_element_type=jnp.float32) * score_scale
+            scores.append(jnp.where(jnp.concatenate(live, axis=1), score, mask_value))
+        row_peak = jnp.max(functools.reduce(jnp.maximum, scores), axis=1, keepdims=True)
         if step == 0:
             recent = lax.dot_general(
                 query, fresh[...], across, preferred_element_type=jnp.float32
             ) * score_scale
             width = recent.shape[1]
             key = lax.broadcasted_iota(jnp.int32, (rows, width), 1)
-            row_step = lax.broadcasted_iota(jnp.int32, (rows, width), 0) // (ranks * heads)
+            row_step = lax.broadcasted_iota(jnp.int32, (rows, width), 0) // half % steps
             seen = (key <= row_step) & (column < 2)
             recent = jnp.where(seen, recent, mask_value)
             row_peak = jnp.maximum(row_peak, jnp.max(recent, axis=1, keepdims=True))
         total, summed = None, None
-        for score, keys in zip(scores, values):
+        for score, key_block in zip(scores, keys):
             weight = jnp.where(score > 0.5 * mask_value, jnp.exp(score - row_peak), 0.0)
             total = weight if total is None else total + weight
             part = lax.dot_general(
-                weight.astype(jnp.bfloat16), keys[0:CKV, :], across, preferred_element_type=jnp.float32
+                weight.astype(jnp.bfloat16), key_block[0:CKV, :], across, preferred_element_type=jnp.float32
             )
             summed = part if summed is None else summed + part
         row_total = jnp.sum(total, axis=1, keepdims=True)
@@ -318,22 +354,26 @@
         extra = jnp.zeros((rows, LANES), jnp.float32)
         for lane, part in enumerate(thirds(row_peak) + thirds(row_total)):
             extra = jnp.where(lanes == lane, part, extra)
-        held[:, 0:CKV] = summed
-        held[:, CKV:] = extra
+        held[step, :, 0:CKV] = summed
+        held[step, :, CKV:] = extra
+    count = steps * half
+    for step in range(ranks):
+        start = pl.multiple_of((me ^ step) * 2 * count, 2 * count)
         for far_step, out in enumerate(out_refs):
             target = me ^ far_step
             block = [
-                held[pl.ds(pl.multiple_of((u * ranks + target) * heads, heads), heads), :]
-                for u in range(steps)
+                held[step, pl.ds(pl.multiple_of((odd * ranks + target) * count, count), count), :]
+                for odd in range(2)
             ]
-            start = pl.multiple_of(rank * steps * heads, steps * heads)
-            out[pl.ds(start, steps * heads), :] = jnp.concatenate(block, axis=0).astype(jnp.bfloat16)
+            out[pl.ds(start, 2 * count), :] = jnp.concatenate(block, axis=0).astype(jnp.bfloat16)
+    fetch.wait()
 
 
 def lift_kernel(heads, ranks, *refs):
     parts, up_value, out, joined, tall = refs[:ranks], refs[ranks], refs[ranks + 1], refs[-2], refs[-1]
     count = parts[0].shape[0]
     rows = count // heads
+    steps, half = rows // ranks, heads // 2
     blocks = [part[...].astype(jnp.float32) for part in parts]
     peaks = [b[:, CKV : CKV + 1] + b[:, CKV + 1 : CKV + 2] + b[:, CKV + 2 : CKV + 3] for b in blocks]
     totals = [b[:, CKV + 3 : CKV + 4] + b[:, CKV + 4 : CKV + 5] + b[:, CKV + 5 : CKV + 6] for b in blocks]
@@ -349,14 +389,21 @@
     tall[...] = jnp.where(lanes < 3 * heads, peak, total)
     lanes = lane_ids(rows)
     extra = jnp.zeros((rows, LANES), jnp.float32)
+
+    def rows_of(read, head):
+        first = (head % 2) * steps * half + head // 2
+        return jnp.concatenate(
+            [read(pl.ds(first + step * half, ranks, stride=steps * heads)) for step in range(steps)], axis=0
+        )
+
     for head in range(heads):
-        pick = pl.ds(head % 2 * (heads // 2) + head // 2, rows, stride=heads)
+        value = jnp.concatenate(
+            [rows_of(lambda at: joined[g, at, :], head) for g in range(CKV // LANES)], axis=1
+        )
         out[:, head * LANES : (head + 1) * LANES] = jnp.dot(
-            jnp.concatenate([joined[g, pick, :] for g in range(CKV // LANES)], axis=1).astype(jnp.bfloat16),
-            up_value[head],
-            preferred_element_type=jnp.float32,
+            value.astype(jnp.bfloat16), up_value[head], preferred_element_type=jnp.float32
         ).astype(jnp.bfloat16)
-        extra = jnp.where(lanes % heads == head, tall[pick, :], extra)
+        extra = jnp.where(lanes % heads == head, rows_of(lambda at: tall[at, :], head), extra)
     high, middle, low = thirds(extra)
     piece = lanes // heads % 3
     out[:, heads * LANES :] = jnp.where(
@@ -364,13 +411,13 @@
     ).astype(jnp.bfloat16)
 
 
-def project_kernel(heads, reps, place, *refs):
+def project_kernel(heads, reps, ranks, *refs):
     parts, (out_proj, residual, sent, kept) = refs[:reps], refs[reps:]
-    core = place[1] % 2
+    me, column = position()
     width = heads * LANES
     rows, steps = kept.shape[0], residual.shape[0]
-    source = lax.broadcasted_iota(jnp.int32, (rows, steps), 0) - place[0] * steps
-    own = source == lax.broadcasted_iota(jnp.int32, (rows, steps), 1)
+    row = lax.broadcasted_iota(jnp.int32, (rows, steps), 0)
+    own = row == lax.broadcasted_iota(jnp.int32, (rows, steps), 1) * ranks + me
     result = jnp.dot(
         own.astype(jnp.bfloat16), residual[...], preferred_element_type=jnp.float32
     )
@@ -384,7 +431,7 @@
 
         peaks = [whole(tail, 0) for tail in tails]
         totals = [whole(tail, 3) for tail in tails]
-        live = lane_ids(result.shape[0]) < heads
+        live = lane_ids(rows) < heads
         peaks = [jnp.where(live, p, 0.0) for p in peaks]
         totals = [jnp.where(live, t, 1.0) for t in totals]
         peak = functools.reduce(jnp.maximum, peaks)
@@ -396,7 +443,7 @@
             lane = slice(head * LANES, (head + 1) * LANES)
             mixed.append(sum(b[:, lane] * f[:, head : head + 1] for b, f in zip(blocks, factors)))
         values = jnp.concatenate(mixed, axis=1).astype(jnp.bfloat16)
-        start = pl.multiple_of((core ^ side) * width, width)
+        start = pl.multiple_of((column % 2 ^ side) * width, width)
         result = result + jnp.dot(
             values, out_proj[pl.ds(start, width), :], preferred_element_type=jnp.float32
         )
@@ -438,17 +485,38 @@
     out[...] = jnp.dot(hidden, w_down[...], preferred_element_type=jnp.float32).astype(jnp.bfloat16)
 
 
-def call(kernel, name, operands, specs, outputs, limit, flops=0, moved=0, scratch=(), out_specs=None):
+def finish_kernel(ranks, mixed, *refs):
+    parts, out = refs[:ranks], refs[ranks]
+    me, _ = position()
+    total = mixed[...]
+    for part in parts:
+        total = total + part[...].astype(jnp.float32)
+    row = lax.broadcasted_iota(jnp.int32, total.shape, 0)
+    picked = [
+        jnp.sum(jnp.where(row == step * ranks + me, total, 0.0), axis=0, keepdims=True)
+        for step in range(out.shape[0])
+    ]
+    out[...] = jnp.concatenate(picked, axis=0).astype(jnp.bfloat16)
+
+
+def call(kernel, operands, specs, outputs, flops=0, moved=0, scratch=(), out_specs=None):
     return pl.pallas_call(
         kernel,
-        name=name,
         out_shape=outputs,
         in_specs=specs,
         out_specs=jax.tree.map(lambda _: vmem(), outputs) if out_specs is None else out_specs,
         scratch_shapes=list(scratch),
-        compiler_params=pltpu.CompilerParams(vmem_limit_bytes=limit),
+        compiler_params=pltpu.CompilerParams(vmem_limit_bytes=6 * MIB),
         cost_estimate=pl.CostEstimate(flops=flops, bytes_accessed=moved, transcendentals=0),
     )(*operands)
+
+
+def in_hbm(*arrays):
+    return [pltpu.with_memory_space_constraint(a, pltpu.HBM) for a in arrays]
+
+
+def hbm():
+    return pl.BlockSpec(memory_space=pltpu.HBM)
 
 
 def shape_of(shape, dtype=jnp.bfloat16):
@@ -471,7 +539,6 @@
     w_down,
 ):
     ranks, reps = lax.axis_size("dp"), lax.axis_size("rep")
-    me, column = lax.axis_index("dp"), lax.axis_index("rep")
     slots = page_rank.shape[1]
     capacity = (slots + ranks - 1) // ranks
     steps, columns = residual.shape
@@ -480,64 +547,62 @@
     heads = head_count // (2 * ranks)
     rows = ranks * steps
     core_pairs = [(i, i ^ 1) for i in range(reps)]
-    place = jnp.stack([me, column])
-
-    share = lax.dynamic_index_in_dim(
-        queries.reshape(steps, ranks, 2, heads * latent), column % 2, 2, keepdims=False
-    ).reshape(rows * heads // 2, 2 * latent)
-    arrived = [share] + partners(share, "dp")
+
+    packed_shape = (rows * heads // 2, 2 * latent)
+    share = call(
+        pack_kernel,
+        in_hbm(queries),
+        [hbm()],
+        shape_of(packed_shape),
+        moved=queries.size * 2,
+        scratch=[
+            pltpu.VMEM((ranks, steps, heads * latent), jnp.bfloat16),
+            pltpu.VMEM(packed_shape, jnp.float32),
+            pltpu.SemaphoreType.DMA((ranks,)),
+        ],
+    )
+    arrived = [share] + partners([share] * ranks, "dp", "query")
     store = latent_store[0]
     far = lax.ppermute(store, "rep", core_pairs)
-    found, near, out_near, up_near = call(
+    found, near, up_near, fresh = call(
         functools.partial(stage_kernel, capacity, heads),
-        "stage",
-        (
-            place,
-            lengths.reshape(ranks),
-            *[pltpu.with_memory_space_constraint(a, pltpu.HBM) for a in (page_rank, page_index, store, out_proj, up_value)],
-        ),
-        [smem()] * 2 + [pl.BlockSpec(memory_space=pltpu.HBM)] * 5,
+        in_hbm(lengths.reshape(ranks), page_rank, page_index, store, up_value, new_latent),
+        [hbm()] * 6,
         [
             shape_of((2 * ranks * capacity,), jnp.int32),
             pltpu.VMEM(store.shape, store.dtype),
-            pltpu.VMEM(out_proj.shape, out_proj.dtype),
             pltpu.VMEM((heads, *up_value.shape[1:]), up_value.dtype),
+            pltpu.VMEM(new_latent.shape, new_latent.dtype),
         ],
-        6 * MIB,
         out_specs=[smem()] + [vmem()] * 3,
-        moved=2 * (store.size + out_proj.size),
+        moved=2 * store.size,
         scratch=[
+            pltpu.SMEM((ranks,), jnp.int32),
             pltpu.SMEM(page_rank.shape, jnp.int32),
             pltpu.SMEM(page_rank.shape, jnp.int32),
-            pltpu.SemaphoreType.DMA((2,)),
+            pltpu.SemaphoreType.DMA((3,)),
             pltpu.SemaphoreType.DMA((3,)),
         ],
     )
     width = CKV + LANES
-    partial_rows = call(
+    *partial_rows, out_near = call(
         functools.partial(attend_kernel, capacity, heads),
-        "attend",
-        (place, found, lax.ppermute(found, "rep", core_pairs), *arrived, near, far, new_latent),
-        [smem()] * 3 + [vmem()] * (ranks + 3),
-        [shape_of((rows * heads, width))] * ranks,
-        6 * MIB,
+        (found, lax.ppermute(found, "rep", core_pairs), *arrived, near, far, fresh, *in_hbm(out_proj)),
+        [smem()] * 2 + [vmem()] * (ranks + 3) + [hbm()],
+        [shape_of((rows * heads, width))] * ranks + [pltpu.VMEM(out_proj.shape, out_proj.dtype)],
+        out_specs=[vmem()] * (ranks + 1),
         scratch=[
-            pltpu.VMEM((rows * heads, latent), jnp.float32),
-            pltpu.VMEM((rows * heads, width), jnp.float32),
+            pltpu.VMEM((ranks, rows * heads, width), jnp.float32),
+            pltpu.SemaphoreType.DMA,
         ],
         flops=2 * 2 * slots * PAGE * rows * heads * latent,
-        moved=2 * near.size * 2,
-    )
-    joined = [partial_rows[0]] + [
-        lax.ppermute(partial_rows[s], "dp", [(i, i ^ s) for i in range(ranks)]) for s in range(1, ranks)
-    ]
+        moved=2 * store.size * 2 + 2 * out_proj.size,
+    )
     lifted = call(
         functools.partial(lift_kernel, heads, ranks),
-        "lift",
-        (*joined, up_near),
+        (partial_rows[0], *partners(partial_rows, "dp", "partial"), up_near),
         [vmem()] * (ranks + 1),
         shape_of((rows, (heads + 1) * LANES)),
-        6 * MIB,
         scratch=[
             pltpu.VMEM((CKV // LANES, rows * heads, LANES), jnp.float32),
             pltpu.VMEM((rows * heads, LANES), jnp.float32),
@@ -546,49 +611,48 @@
         moved=up_near.size * 2,
     )
     sent, kept = call(
-        functools.partial(project_kernel, heads, reps),
-        "project",
-        (place, lifted, *partners(lifted, "rep"), out_near, residual),
-        [smem()] + [vmem()] * (reps + 2),
+        functools.partial(project_kernel, heads, reps, ranks),
+        (lifted, *partners([lifted] * reps, "rep", "lifted"), out_near, residual),
+        [vmem()] * (reps + 2),
         [shape_of((rows, columns)), shape_of((rows, columns), jnp.float32)],
-        6 * MIB,
         flops=2 * rows * out_proj.size,
         moved=out_proj.size * 2,
     )
     gate_up, mixed = call(
         functools.partial(gate_kernel, ranks),
-        "gate",
-        (kept, *partners(sent, "dp"), norm_gain.reshape(1, columns), w_gate, w_up),
+        (kept, *partners([sent] * ranks, "dp", "mixed"), norm_gain.reshape(1, columns), w_gate, w_up),
         [vmem()] * (ranks + 3),
         [shape_of((rows, 2 * w_gate.shape[1] + LANES)), shape_of((rows, columns), jnp.float32)],
-        6 * MIB,
         flops=4 * rows * w_gate.size,
         moved=w_gate.size * 4,
     )
     down = call(
         functools.partial(down_kernel, reps, columns * reps),
-        "down",
-        (gate_up, *partners(gate_up, "rep"), w_down),
+        (gate_up, *partners([gate_up] * reps, "rep", "units"), w_down),
         [vmem()] * (reps + 1),
         shape_of((rows, columns)),
-        6 * MIB,
         flops=2 * rows * w_down.size,
         moved=w_down.size * 2,
     )
-
-    def mine(array):
-        return lax.dynamic_slice_in_dim(array, me * steps, steps).astype(jnp.float32)
-
-    return (mine(mixed) + sum(mine(a) for a in [down] + partners(down, "dp"))).astype(jnp.bfloat16)
+    return call(
+        functools.partial(finish_kernel, ranks),
+        (mixed, down, *partners([down] * ranks, "dp", "down")),
+        [vmem()] * (ranks + 1),
+        shape_of((steps, columns)),
+        moved=rows * columns * 12,
+    )
+
+
+def share_of_latent_work(mesh):
+    return mesh.shape["dp"] <= 8 and mesh.shape["rep"] % 2 == 0
 
 
 def on_device(*arrays):
-    ranks = lax.axis_size("dp")
     lengths, queries, new_latent = arrays[3:6]
     heads = queries.shape[1] // new_latent.shape[1]
-    if ranks <= 8 and heads % (16 * ranks) == 0 and lengths.shape[1] == 1:
-        return queries_moved(*arrays)
-    return pages_moved(*arrays)
+    if heads % (16 * lax.axis_size("dp")) or lengths.shape[1] != 1:
+        raise ValueError("unsupported shapes")
+    return queries_moved(*arrays)
 
 
 def solution(mesh):
@@ -608,6 +672,11 @@
         P("dp", "rep"),
     )
     out_specs = P(("groups", "dp"), "rep")
+    moves = share_of_latent_work(mesh)
     return jax.shard_map(
-        on_device, mesh=mesh, in_specs=in_specs, out_specs=out_specs, check_vma=False
-    )
+        on_device if moves else pages_moved,
+        mesh=mesh,
+        in_specs=in_specs,
+        out_specs=out_specs,
+        check_vma=False,
+    )

time: 65.4 us -> 66.1 us (1.011)
  local copies, waits for them, and re-layouts: 2.24 us -> 0.05 us
  waiting for transfers between devices: 23.5 us -> 25.6 us
  Pallas kernels: 15.4 us -> 17.1 us
  other arithmetic: 0.71 us -> 0.01 us
    ppermute x18, waiting for transfers between devices: 22.4 us -> 24.4 us  [partners(): lax.ppermute(arrays[step], axis, [(i, i ^ step) for i in range(size)])]
    pallas_call x6 -> x8, Pallas kernels: 15.4 us -> 17.1 us  [call(): pl.pallas_call(kernel, out_shape=outputs, in_specs=specs, out_specs=jax.t...]
    reshape x2 -> x0, local copies, waits for them, and re-layouts: 1.08 us -> none  [the longest x1 1.03 us: queries_moved(): queries.reshape(steps, ranks, 2, heads * latent)]
  transfers between devices with their start and end apart: 20 -> 20, of which waited for: 11 -> 12; matrix products, arithmetic and copies ran while one was open for 2% -> 0% of each run, Pallas kernels for 8% -> 5%
where the time goes in v3:
time: 66.1 us; the launch traced here: 65.9 us
  waiting for transfers between devices  25.6 us (39%)
  starting transfers between devices  23.1 us (35%)
  Pallas kernels  17.1 us (26%)
    ppermute x18, waiting for transfers between devices, partners(): lax.ppermute(arrays[step], axis, [(i, i ^ step) for i in range(size)])  24.4 us
    ppermute x18, starting transfers between devices, partners(): lax.ppermute(arrays[step], axis, [(i, i ^ step) for i in range(size)])  22.5 us
    pallas_call x8, Pallas kernels, call(): pl.pallas_call(kernel, out_shape=outputs, in_specs=specs, out_specs=jax.t...  17.1 us
  transfers between devices with their start and end apart: 20, of which 12 were waited for; matrix products, arithmetic and copies ran while one was open for 0% of the time, Pallas kernels for 5%

profile of v3, /device:TPU:0, one launch (start us, length us, event | category | flops | bytes accessed | tf_op | source)
XLA Modules:
  0.0 65.9 jit_solution(8080799399932080896)
XLA Ops:
  0.0 0.5 collective-permute-start.4
  0.5 0.8 %shard_map.128.refs_0_ = bf16[32,1152]{1,0:T(8,128)(2,1)S(1)} custom-call(bf16[2,36864]{1,0:T(2,128)(2,1)} %queries.1), custom_call_target="tpu_custom_call" | custom-call | bytes 147456 | tf_op jit(solution)/shard_map/pallas_call | solution.py:503
  1.3 2.6 %collective-permute-start.1 = (bf16[32,1152]{1,0:T(8,128)(2,1)S(1)}, bf16[32,1152]{1,0:T(8,128)(2,1)S(1)}, u32[]{:S(2)}, u32[]{:S(2)}) collective-permute-start(bf16[32,1152]{1,0:T(8,128)(2,1)S(1)} %shard_map.128.refs_0_), channel_id=1, source_target_pairs={{0,4},{4,0},{8,12},{12,8},{1,5},{5,1},{9,13},{13,9},{2,6},{6,2},{1... | collective-permute-start | bytes 221192 | tf_op jit(solution)/shard_map/ppermute | solution.py:211
  4.0 2.6 %collective-permute-start.2 = (bf16[32,1152]{1,0:T(8,128)(2,1)S(1)}, bf16[32,1152]{1,0:T(8,128)(2,1)S(1)}, u32[]{:S(2)}, u32[]{:S(2)}) collective-permute-start(bf16[32,1152]{1,0:T(8,128)(2,1)S(1)} %shard_map.128.refs_0_), channel_id=1, source_target_pairs={{0,8},{4,12},{8,0},{12,4},{1,9},{5,13},{9,1},{13,5},{2,10},{6,14},... | collective-permute-start | bytes 221192 | tf_op jit(solution)/shard_map/ppermute | solution.py:211
  6.5 0.0 collective-permute-start.3
  6.5 0.0 copy-start.1
  6.6 0.0 slice-start
  6.6 2.6 %shard_map.127 = (s32[24]{0:T(128)S(1)}, bf16[12,576,128]{2,1,0:T(8,128)(2,1)S(1)}, bf16[8,512,128]{2,1,0:T(8,128)(2,1)S(1)}, bf16[2,576]{1,0:T(2,128)(2,1)S(1)}) custom-call(s32[4]{0:T(128)} %bitcast.8, s32[4,12]{1,0:T(4,128)} %rank_hbm.1, s32[4,12]{1,0:T(4,128)} %index_hbm.1, bf16[12,576,128]{2,1,0:T(8,128)(2,1)} %bitcast.7, ...), custom_call_target="tpu_custom_call" | custom-call | bytes 1769472 | tf_op jit(solution)/shard_map/pallas_call | solution.py:503
  9.1 0.1 collective-permute-start
  9.2 1.1 %collective-permute-done.far_list = s32[24]{0:T(128)S(1)} collective-permute-done((s32[24]{0:T(128)S(1)}, s32[24]{0:T(128)S(1)}, u32[]{:S(2)}, u32[]{:S(2)}) %collective-permute-start) | collective-permute-done | bytes 128 | tf_op jit(solution)/shard_map/ppermute | solution.py:590
  10.3 0.0 collective-permute-done.1.refs_1_
  10.3 2.5 %collective-permute-done.2.refs_2_ = bf16[32,1152]{1,0:T(8,128)(2,1)S(1)} collective-permute-done((bf16[32,1152]{1,0:T(8,128)(2,1)S(1)}, bf16[32,1152]{1,0:T(8,128)(2,1)S(1)}, u32[]{:S(2)}, u32[]{:S(2)}) %collective-permute-start.2) | collective-permute-done | bytes 73760 | tf_op jit(solution)/shard_map/ppermute | solution.py:211
  12.9 0.0 collective-permute-done.3.refs_3_
  12.9 0.0 collective-permute-done.4.refs_5_
  12.9 0.0 copy-start.2
  12.9 0.0 slice-start.1
  12.9 0.0 copy-start
  12.9 6.8 %shard_map.129 = (bf16[64,640]{1,0:T(8,128)(2,1)S(1)}, bf16[64,640]{1,0:T(8,128)(2,1)S(1)}, bf16[64,640]{1,0:T(8,128)(2,1)S(1)}, bf16[64,640]{1,0:T(8,128)(2,1)S(1)}, bf16[2048,1792]{1,0:T(8,128)(2,1)S(1)}) custom-call(s32[24]{0:T(128)S(1)} %get-tuple-element.18.near_list, s32[24]{0:T(128)S(1)} %collective-permute-done.far_list, ...), custom_call_target="tpu_custom_call" | custom-call | flops 226492416 | bytes 10878976 | tf_op jit(solution)/shard_map/pallas_call | solution.py:503
  19.7 1.7 %collective-permute-start.5 = (bf16[64,640]{1,0:T(8,128)(2,1)S(1)}, bf16[64,640]{1,0:T(8,128)(2,1)S(1)}, u32[]{:S(2)}, u32[]{:S(2)}) collective-permute-start(bf16[64,640]{1,0:T(8,128)(2,1)S(1)} %get-tuple-element.22), channel_id=1, source_target_pairs={{0,4},{4,0},{8,12},{12,8},{1,5},{5,1},{9,13},{13,9},{2,6},{6,2},{1... | collective-permute-start | bytes 245768 | tf_op jit(solution)/shard_map/ppermute | solution.py:211
  21.4 1.6 %collective-permute-start.6 = (bf16[64,640]{1,0:T(8,128)(2,1)S(1)}, bf16[64,640]{1,0:T(8,128)(2,1)S(1)}, u32[]{:S(2)}, u32[]{:S(2)}) collective-permute-start(bf16[64,640]{1,0:T(8,128)(2,1)S(1)} %get-tuple-element.23), channel_id=1, source_target_pairs={{0,8},{4,12},{8,0},{12,4},{1,9},{5,13},{9,1},{13,5},{2,10},{6,14},... | collective-permute-start | bytes 245768 | tf_op jit(solution)/shard_map/ppermute | solution.py:211
  23.1 1.1 %collective-permute-start.7 = (bf16[64,640]{1,0:T(8,128)(2,1)S(1)}, bf16[64,640]{1,0:T(8,128)(2,1)S(1)}, u32[]{:S(2)}, u32[]{:S(2)}) collective-permute-start(bf16[64,640]{1,0:T(8,128)(2,1)S(1)} %get-tuple-element.24), channel_id=1, source_target_pairs={{0,12},{4,8},{8,4},{12,0},{1,13},{5,9},{9,5},{13,1},{2,14},{6,10},... | collective-permute-start | bytes 245768 | tf_op jit(solution)/shard_map/ppermute | solution.py:211
  24.1 0.1 collective-permute-done.5.refs_1_
  24.3 6.0 %collective-permute-done.6.refs_2_ = bf16[64,640]{1,0:T(8,128)(2,1)S(1)} collective-permute-done((bf16[64,640]{1,0:T(8,128)(2,1)S(1)}, bf16[64,640]{1,0:T(8,128)(2,1)S(1)}, u32[]{:S(2)}, u32[]{:S(2)}) %collective-permute-start.6) | collective-permute-done | bytes 81952 | tf_op jit(solution)/shard_map/ppermute | solution.py:211
  30.3 0.0 collective-permute-done.7.refs_3_
  30.3 0.5 shard_map.130.refs_0_
  30.8 0.1 collective-permute-start.10
  30.8 1.6 %collective-permute-start.8 = (bf16[8,1152]{1,0:T(8,128)(2,1)S(1)}, bf16[8,1152]{1,0:T(8,128)(2,1)S(1)}, u32[]{:S(2)}, u32[]{:S(2)}) collective-permute-start(bf16[8,1152]{1,0:T(8,128)(2,1)S(1)} %shard_map.130.refs_0_), channel_id=1, source_target_pairs={{0,1},{1,0},{2,3},{3,2},{4,5},{5,4},{6,7},{7,6},{8,9},{9,8},{10,11... | collective-permute-start | bytes 55304 | tf_op jit(solution)/shard_map/ppermute | solution.py:211
  32.4 0.5 collective-permute-start.9
  33.0 1.2 %collective-permute-done.10.refs_3_ = bf16[8,1152]{1,0:T(8,128)(2,1)S(1)} collective-permute-done((bf16[8,1152]{1,0:T(8,128)(2,1)S(1)}, bf16[8,1152]{1,0:T(8,128)(2,1)S(1)}, u32[]{:S(2)}, u32[]{:S(2)}) %collective-permute-start.10) | collective-permute-done | bytes 18464 | tf_op jit(solution)/shard_map/ppermute | solution.py:211
  34.1 0.0 collective-permute-done.8.refs_1_
  34.1 2.0 %collective-permute-done.9.refs_2_ = bf16[8,1152]{1,0:T(8,128)(2,1)S(1)} collective-permute-done((bf16[8,1152]{1,0:T(8,128)(2,1)S(1)}, bf16[8,1152]{1,0:T(8,128)(2,1)S(1)}, u32[]{:S(2)}, u32[]{:S(2)}) %collective-permute-start.9) | collective-permute-done | bytes 18464 | tf_op jit(solution)/shard_map/ppermute | solution.py:211
  36.2 0.0 copy-done.1
  36.2 1.2 %shard_map.131 = (bf16[8,1792]{1,0:T(8,128)(2,1)S(1)}, f32[8,1792]{1,0:T(8,128)S(1)}) custom-call(bf16[8,1152]{1,0:T(8,128)(2,1)S(1)} %shard_map.130.refs_0_, bf16[8,1152]{1,0:T(8,128)(2,1)S(1)} %collective-permute-done.8.refs_1_, bf16[8,1152]{1,0:T(8,128)(2,1)S(1)} %collective-permute-done.9.refs_2_, bf16[8,1152]{1,0:T(8,128)(2,1)S(1)} %collective-permute-done.10.refs_3_, ...), custom_call_target="tpu_custom_call" | custom-call | flops 58720256 | bytes 7340032 | tf_op jit(solution)/shard_map/pallas_call | solution.py:503
  37.4 1.6 %collective-permute-start.11 = (bf16[8,1792]{1,0:T(8,128)(2,1)S(1)}, bf16[8,1792]{1,0:T(8,128)(2,1)S(1)}, u32[]{:S(2)}, u32[]{:S(2)}) collective-permute-start(bf16[8,1792]{1,0:T(8,128)(2,1)S(1)} %get-tuple-element.28), channel_id=1, source_target_pairs={{0,4},{4,0},{8,12},{12,8},{1,5},{5,1},{9,13},{13,9},{2,6},{6,2},{1... | collective-permute-start | bytes 86024 | tf_op jit(solution)/shard_map/ppermute | solution.py:211
  39.0 1.1 %collective-permute-start.12 = (bf16[8,1792]{1,0:T(8,128)(2,1)S(1)}, bf16[8,1792]{1,0:T(8,128)(2,1)S(1)}, u32[]{:S(2)}, u32[]{:S(2)}) collective-permute-start(bf16[8,1792]{1,0:T(8,128)(2,1)S(1)} %get-tuple-element.28), channel_id=1, source_target_pairs={{0,8},{4,12},{8,0},{12,4},{1,9},{5,13},{9,1},{13,5},{2,10},{6,14},... | collective-permute-start | bytes 86024 | tf_op jit(solution)/shard_map/ppermute | solution.py:211
  40.1 1.7 %collective-permute-start.13 = (bf16[8,1792]{1,0:T(8,128)(2,1)S(1)}, bf16[8,1792]{1,0:T(8,128)(2,1)S(1)}, u32[]{:S(2)}, u32[]{:S(2)}) collective-permute-start(bf16[8,1792]{1,0:T(8,128)(2,1)S(1)} %get-tuple-element.28), channel_id=1, source_target_pairs={{0,12},{4,8},{8,4},{12,0},{1,13},{5,9},{9,5},{13,1},{2,14},{6,10},... | collective-permute-start | bytes 86024 | tf_op jit(solution)/shard_map/ppermute | solution.py:211
  41.8 0.0 copy-done.2
  41.8 0.0 collective-permute-done.11.refs_1_
  41.8 2.1 %collective-permute-done.12.refs_2_ = bf16[8,1792]{1,0:T(8,128)(2,1)S(1)} collective-permute-done((bf16[8,1792]{1,0:T(8,128)(2,1)S(1)}, bf16[8,1792]{1,0:T(8,128)(2,1)S(1)}, u32[]{:S(2)}, u32[]{:S(2)}) %collective-permute-start.12) | collective-permute-done | bytes 28704 | tf_op jit(solution)/shard_map/ppermute | solution.py:211
  43.9 1.8 %collective-permute-done.13.refs_3_ = bf16[8,1792]{1,0:T(8,128)(2,1)S(1)} collective-permute-done((bf16[8,1792]{1,0:T(8,128)(2,1)S(1)}, bf16[8,1792]{1,0:T(8,128)(2,1)S(1)}, u32[]{:S(2)}, u32[]{:S(2)}) %collective-permute-start.13) | collective-permute-done | bytes 28704 | tf_op jit(solution)/shard_map/ppermute | solution.py:211
  45.8 0.0 slice-done
  45.8 0.0 slice-done.1
  45.8 0.0 copy-done
  45.8 0.0 slice-done.2
  45.8 0.0 slice-start.4
  45.8 0.0 slice-start.5
  45.8 3.0 %shard_map.132 = (bf16[8,6272]{1,0:T(8,128)(2,1)S(1)}, f32[8,1792]{1,0:T(8,128)S(1)}) custom-call(f32[8,1792]{1,0:T(8,128)S(1)} %get-tuple-element.27.refs_0_, bf16[8,1792]{1,0:T(8,128)(2,1)S(1)} %collective-permute-done.11.refs_1_, bf16[8,1792]{1,0:T(8,128)(2,1)S(1)} %collective-permute-done.12.refs_2_, ...), custom_call_target="tpu_custom_call" | custom-call | flops 176160768 | bytes 22020096 | tf_op jit(solution)/shard_map/pallas_call | solution.py:503
  48.8 0.0 collective-permute-start.14
  48.8 0.6 collective-permute-start.15
  49.4 1.3 %collective-permute-start.16 = (bf16[8,6272]{1,0:T(8,128)(2,1)S(1)}, bf16[8,6272]{1,0:T(8,128)(2,1)S(1)}, u32[]{:S(2)}, u32[]{:S(2)}) collective-permute-start(bf16[8,6272]{1,0:T(8,128)(2,1)S(1)} %get-tuple-element.30.refs_0_), channel_id=1, source_target_pairs={{0,3},{1,2},{2,1},{3,0},{4,7},{5,6},{6,5},{7,4},{8,11},{9,10},{10,... | collective-permute-start | bytes 301064 | tf_op jit(solution)/shard_map/ppermute | solution.py:211
  50.6 0.0 collective-permute-done.14.refs_1_
  50.7 3.9 %collective-permute-done.15.refs_2_ = bf16[8,6272]{1,0:T(8,128)(2,1)S(1)} collective-permute-done((bf16[8,6272]{1,0:T(8,128)(2,1)S(1)}, bf16[8,6272]{1,0:T(8,128)(2,1)S(1)}, u32[]{:S(2)}, u32[]{:S(2)}) %collective-permute-start.15) | collective-permute-done | bytes 100384 | tf_op jit(solution)/shard_map/ppermute | solution.py:211
  54.5 1.1 %collective-permute-done.16.refs_3_ = bf16[8,6272]{1,0:T(8,128)(2,1)S(1)} collective-permute-done((bf16[8,6272]{1,0:T(8,128)(2,1)S(1)}, bf16[8,6272]{1,0:T(8,128)(2,1)S(1)}, u32[]{:S(2)}, u32[]{:S(2)}) %collective-permute-start.16) | collective-permute-done | bytes 100384 | tf_op jit(solution)/shard_map/ppermute | solution.py:211
  55.7 0.0 slice-done.3
  55.7 0.0 slice-done.4
  55.7 0.0 slice-done.5
  55.7 1.6 %shard_map.133.refs_0_ = bf16[8,1792]{1,0:T(8,128)(2,1)S(1)} custom-call(bf16[8,6272]{1,0:T(8,128)(2,1)S(1)} %get-tuple-element.30.refs_0_, bf16[8,6272]{1,0:T(8,128)(2,1)S(1)} %collective-permute-done.14.refs_1_, bf16[8,6272]{1,0:T(8,128)(2,1)S(1)} %collective-permute-done.15.refs_2_, bf16[8,6272]{1,0:T(8,128)(2,1)S(1)} %collective-permute-done.16.refs_3_, ...), custom_call_target="tpu_custom_call" | custom-call | flops 88080384 | bytes 11010048 | tf_op jit(solution)/shard_map/pallas_call | solution.py:503
  57.3 0.0 collective-permute-start.17
  57.3 2.3 %collective-permute-start.18 = (bf16[8,1792]{1,0:T(8,128)(2,1)S(1)}, bf16[8,1792]{1,0:T(8,128)(2,1)S(1)}, u32[]{:S(2)}, u32[]{:S(2)}) collective-permute-start(bf16[8,1792]{1,0:T(8,128)(2,1)S(1)} %shard_map.133.refs_0_), channel_id=1, source_target_pairs={{0,8},{4,12},{8,0},{12,4},{1,9},{5,13},{9,1},{13,5},{2,10},{6,14},... | collective-permute-start | bytes 86024 | tf_op jit(solution)/shard_map/ppermute | solution.py:211
  59.6 2.1 %collective-permute-start.19 = (bf16[8,1792]{1,0:T(8,128)(2,1)S(1)}, bf16[8,1792]{1,0:T(8,128)(2,1)S(1)}, u32[]{:S(2)}, u32[]{:S(2)}) collective-permute-start(bf16[8,1792]{1,0:T(8,128)(2,1)S(1)} %shard_map.133.refs_0_), channel_id=1, source_target_pairs={{0,12},{4,8},{8,4},{12,0},{1,13},{5,9},{9,5},{13,1},{2,14},{6,10},... | collective-permute-start | bytes 86024 | tf_op jit(solution)/shard_map/ppermute | solution.py:211
  61.7 0.0 collective-permute-done.17.refs_1_
  61.7 0.6 collective-permute-done.18.refs_2_
  62.3 2.9 %collective-permute-done.19.refs_3_ = bf16[8,1792]{1,0:T(8,128)(2,1)S(1)} collective-permute-done((bf16[8,1792]{1,0:T(8,128)(2,1)S(1)}, bf16[8,1792]{1,0:T(8,128)(2,1)S(1)}, u32[]{:S(2)}, u32[]{:S(2)}) %collective-permute-start.19) | collective-permute-done | bytes 28704 | tf_op jit(solution)/shard_map/ppermute | solution.py:211
  65.3 0.7 shard_map.134
  (5 shorter events, 0.0 us)
Async XLA Ops:
  0.0 12.9 %collective-permute-start.4 = (bf16[12,576,128]{2,1,0:T(8,128)(2,1)}, bf16[12,576,128]{2,1,0:T(8,128)(2,1)S(1)}, u32[]{:S(2)}, u32[]{:S(2)}) collective-permute-start(bf16[12,576,128]{2,1,0:T(8,128)(2,1)} %bitcast.6), channel_id=1, source_target_pairs={{0,1},{1,0},{2,3},{3,2},{4,5},{5,4},{6,7},{7,6},{8,9},{9,8},{10,11... | collective-permute-start | bytes 5308424 | tf_op jit(solution)/shard_map/ppermute | solution.py:566
  1.3 9.0 %collective-permute-start.1 = (bf16[32,1152]{1,0:T(8,128)(2,1)S(1)}, bf16[32,1152]{1,0:T(8,128)(2,1)S(1)}, u32[]{:S(2)}, u32[]{:S(2)}) collective-permute-start(bf16[32,1152]{1,0:T(8,128)(2,1)S(1)} %shard_map.128.refs_0_), channel_id=1, source_target_pairs={{0,4},{4,0},{8,12},{12,8},{1,5},{5,1},{9,13},{13,9},{2,6},{6,2},{1... | collective-permute-start | bytes 221192 | tf_op jit(solution)/shard_map/ppermute | solution.py:211
  4.0 8.9 %collective-permute-start.2 = (bf16[32,1152]{1,0:T(8,128)(2,1)S(1)}, bf16[32,1152]{1,0:T(8,128)(2,1)S(1)}, u32[]{:S(2)}, u32[]{:S(2)}) collective-permute-start(bf16[32,1152]{1,0:T(8,128)(2,1)S(1)} %shard_map.128.refs_0_), channel_id=1, source_target_pairs={{0,8},{4,12},{8,0},{12,4},{1,9},{5,13},{9,1},{13,5},{2,10},{6,14},... | collective-permute-start | bytes 221192 | tf_op jit(solution)/shard_map/ppermute | solution.py:211
  6.5 6.3 %collective-permute-start.3 = (bf16[32,1152]{1,0:T(8,128)(2,1)S(1)}, bf16[32,1152]{1,0:T(8,128)(2,1)S(1)}, u32[]{:S(2)}, u32[]{:S(2)}) collective-permute-start(bf16[32,1152]{1,0:T(8,128)(2,1)S(1)} %shard_map.128.refs_0_), channel_id=1, source_target_pairs={{0,12},{4,8},{8,4},{12,0},{1,13},{5,9},{9,5},{13,1},{2,14},{6,10},... | collective-permute-start | bytes 221192 | tf_op jit(solution)/shard_map/ppermute | solution.py:211
  6.5 29.6 %copy-start.1 = (bf16[2,1792]{1,0:T(2,128)(2,1)S(1)}, bf16[2,1792]{1,0:T(2,128)(2,1)}, u32[]{:S(2)}) copy-start(bf16[2,1792]{1,0:T(2,128)(2,1)} %refs_5_.2) | copy-start | bytes 21508
  6.6 39.2 %slice-start = ((s8[11010048]{0:T(1024)(128)(4,1)}), s8[4194304]{0:T(1024)(128)(4,1)S(1)}, s32[]{:S(2)}) async-start(s8[11010048]{0:T(1024)(128)(4,1)} %bitcast.2), calls=%async_computation | async-start | bytes 8388608
  9.1 1.2 %collective-permute-start = (s32[24]{0:T(128)S(1)}, s32[24]{0:T(128)S(1)}, u32[]{:S(2)}, u32[]{:S(2)}) collective-permute-start(s32[24]{0:T(128)S(1)} %get-tuple-element.18.near_list), channel_id=1, source_target_pairs={{0,1},{1,0},{2,3},{3,2},{4,5},{5,4},{6,7},{7,6},{8,9},{9,8},{10,11... | collective-permute-start | bytes 296 | tf_op jit(solution)/shard_map/ppermute | solution.py:590
  12.9 28.9 %copy-start.2 = (f32[1792]{0:T(1024)S(1)}, f32[1792]{0:T(1024)}, u32[]{:S(2)}) copy-start(f32[1792]{0:T(1024)} %param.22) | copy-start | bytes 21508
  12.9 32.9 %slice-start.1 = ((s8[11010048]{0:T(1024)(128)(4,1)}), s8[4194304]{0:T(1024)(128)(4,1)S(1)}, s32[]{:S(2)}) async-start(s8[11010048]{0:T(1024)(128)(4,1)} %bitcast.2), calls=%async_computation.1 | async-start | bytes 8388608
  12.9 32.9 %copy-start = (bf16[1792,3072]{1,0:T(8,128)(2,1)S(1)}, bf16[1792,3072]{1,0:T(8,128)(2,1)}, u32[]{:S(2)}) copy-start(bf16[1792,3072]{1,0:T(8,128)(2,1)} %refs_6_.1) | copy-start | bytes 33030148
  19.7 4.6 %collective-permute-start.5 = (bf16[64,640]{1,0:T(8,128)(2,1)S(1)}, bf16[64,640]{1,0:T(8,128)(2,1)S(1)}, u32[]{:S(2)}, u32[]{:S(2)}) collective-permute-start(bf16[64,640]{1,0:T(8,128)(2,1)S(1)} %get-tuple-element.22), channel_id=1, source_target_pairs={{0,4},{4,0},{8,12},{12,8},{1,5},{5,1},{9,13},{13,9},{2,6},{6,2},{1... | collective-permute-start | bytes 245768 | tf_op jit(solution)/shard_map/ppermute | solution.py:211
  21.4 8.8 %collective-permute-start.6 = (bf16[64,640]{1,0:T(8,128)(2,1)S(1)}, bf16[64,640]{1,0:T(8,128)(2,1)S(1)}, u32[]{:S(2)}, u32[]{:S(2)}) collective-permute-start(bf16[64,640]{1,0:T(8,128)(2,1)S(1)} %get-tuple-element.23), channel_id=1, source_target_pairs={{0,8},{4,12},{8,0},{12,4},{1,9},{5,13},{9,1},{13,5},{2,10},{6,14},... | collective-permute-start | bytes 245768 | tf_op jit(solution)/shard_map/ppermute | solution.py:211
  23.1 7.2 %collective-permute-start.7 = (bf16[64,640]{1,0:T(8,128)(2,1)S(1)}, bf16[64,640]{1,0:T(8,128)(2,1)S(1)}, u32[]{:S(2)}, u32[]{:S(2)}) collective-permute-start(bf16[64,640]{1,0:T(8,128)(2,1)S(1)} %get-tuple-element.24), channel_id=1, source_target_pairs={{0,12},{4,8},{8,4},{12,0},{1,13},{5,9},{9,5},{13,1},{2,14},{6,10},... | collective-permute-start | bytes 245768 | tf_op jit(solution)/shard_map/ppermute | solution.py:211
  30.3 15.5 %slice-start.2 = ((s8[11010048]{0:T(1024)(128)(4,1)}), s8[2621440]{0:T(1024)(128)(4,1)S(1)}, s32[]{:S(2)}) async-start(s8[11010048]{0:T(1024)(128)(4,1)} %bitcast.2), calls=%async_computation.2 | async-start | bytes 5242880
  30.8 3.4 %collective-permute-start.10 = (bf16[8,1152]{1,0:T(8,128)(2,1)S(1)}, bf16[8,1152]{1,0:T(8,128)(2,1)S(1)}, u32[]{:S(2)}, u32[]{:S(2)}) collective-permute-start(bf16[8,1152]{1,0:T(8,128)(2,1)S(1)} %shard_map.130.refs_0_), channel_id=1, source_target_pairs={{0,3},{1,2},{2,1},{3,0},{4,7},{5,6},{6,5},{7,4},{8,11},{9,10},{10,... | collective-permute-start | bytes 55304 | tf_op jit(solution)/shard_map/ppermute | solution.py:211
  30.8 3.3 %collective-permute-start.8 = (bf16[8,1152]{1,0:T(8,128)(2,1)S(1)}, bf16[8,1152]{1,0:T(8,128)(2,1)S(1)}, u32[]{:S(2)}, u32[]{:S(2)}) collective-permute-start(bf16[8,1152]{1,0:T(8,128)(2,1)S(1)} %shard_map.130.refs_0_), channel_id=1, source_target_pairs={{0,1},{1,0},{2,3},{3,2},{4,5},{5,4},{6,7},{7,6},{8,9},{9,8},{10,11... | collective-permute-start | bytes 55304 | tf_op jit(solution)/shard_map/ppermute | solution.py:211
  32.4 3.8 %collective-permute-start.9 = (bf16[8,1152]{1,0:T(8,128)(2,1)S(1)}, bf16[8,1152]{1,0:T(8,128)(2,1)S(1)}, u32[]{:S(2)}, u32[]{:S(2)}) collective-permute-start(bf16[8,1152]{1,0:T(8,128)(2,1)S(1)} %shard_map.130.refs_0_), channel_id=1, source_target_pairs={{0,2},{1,3},{2,0},{3,1},{4,6},{5,7},{6,4},{7,5},{8,10},{9,11},{10,... | collective-permute-start | bytes 55304 | tf_op jit(solution)/shard_map/ppermute | solution.py:211
  37.4 4.4 %collective-permute-start.11 = (bf16[8,1792]{1,0:T(8,128)(2,1)S(1)}, bf16[8,1792]{1,0:T(8,128)(2,1)S(1)}, u32[]{:S(2)}, u32[]{:S(2)}) collective-permute-start(bf16[8,1792]{1,0:T(8,128)(2,1)S(1)} %get-tuple-element.28), channel_id=1, source_target_pairs={{0,4},{4,0},{8,12},{12,8},{1,5},{5,1},{9,13},{13,9},{2,6},{6,2},{1... | collective-permute-start | bytes 86024 | tf_op jit(solution)/shard_map/ppermute | solution.py:211
  39.0 4.9 %collective-permute-start.12 = (bf16[8,1792]{1,0:T(8,128)(2,1)S(1)}, bf16[8,1792]{1,0:T(8,128)(2,1)S(1)}, u32[]{:S(2)}, u32[]{:S(2)}) collective-permute-start(bf16[8,1792]{1,0:T(8,128)(2,1)S(1)} %get-tuple-element.28), channel_id=1, source_target_pairs={{0,8},{4,12},{8,0},{12,4},{1,9},{5,13},{9,1},{13,5},{2,10},{6,14},... | collective-permute-start | bytes 86024 | tf_op jit(solution)/shard_map/ppermute | solution.py:211
  40.1 5.7 %collective-permute-start.13 = (bf16[8,1792]{1,0:T(8,128)(2,1)S(1)}, bf16[8,1792]{1,0:T(8,128)(2,1)S(1)}, u32[]{:S(2)}, u32[]{:S(2)}) collective-permute-start(bf16[8,1792]{1,0:T(8,128)(2,1)S(1)} %get-tuple-element.28), channel_id=1, source_target_pairs={{0,12},{4,8},{8,4},{12,0},{1,13},{5,9},{9,5},{13,1},{2,14},{6,10},... | collective-permute-start | bytes 86024 | tf_op jit(solution)/shard_map/ppermute | solution.py:211
  45.8 9.9 %slice-start.3 = ((s8[11010048]{0:T(1024)(128)(4,1)}), s8[4194304]{0:T(1024)(128)(4,1)S(1)}, s32[]{:S(2)}) async-start(s8[11010048]{0:T(1024)(128)(4,1)} %bitcast.4), calls=%async_computation.3 | async-start | bytes 8388608
  45.8 9.9 %slice-start.4 = ((s8[11010048]{0:T(1024)(128)(4,1)}), s8[4194304]{0:T(1024)(128)(4,1)S(1)}, s32[]{:S(2)}) async-start(s8[11010048]{0:T(1024)(128)(4,1)} %bitcast.4), calls=%async_computation.4 | async-start | bytes 8388608
  45.8 9.9 %slice-start.5 = ((s8[11010048]{0:T(1024)(128)(4,1)}), s8[2621440]{0:T(1024)(128)(4,1)S(1)}, s32[]{:S(2)}) async-start(s8[11010048]{0:T(1024)(128)(4,1)} %bitcast.4), calls=%async_computation.5 | async-start | bytes 5242880
  48.8 1.9 %collective-permute-start.14 = (bf16[8,6272]{1,0:T(8,128)(2,1)S(1)}, bf16[8,6272]{1,0:T(8,128)(2,1)S(1)}, u32[]{:S(2)}, u32[]{:S(2)}) collective-permute-start(bf16[8,6272]{1,0:T(8,128)(2,1)S(1)} %get-tuple-element.30.refs_0_), channel_id=1, source_target_pairs={{0,1},{1,0},{2,3},{3,2},{4,5},{5,4},{6,7},{7,6},{8,9},{9,8},{10,11... | collective-permute-start | bytes 301064 | tf_op jit(solution)/shard_map/ppermute | solution.py:211
  48.8 5.8 %collective-permute-start.15 = (bf16[8,6272]{1,0:T(8,128)(2,1)S(1)}, bf16[8,6272]{1,0:T(8,128)(2,1)S(1)}, u32[]{:S(2)}, u32[]{:S(2)}) collective-permute-start(bf16[8,6272]{1,0:T(8,128)(2,1)S(1)} %get-tuple-element.30.refs_0_), channel_id=1, source_target_pairs={{0,2},{1,3},{2,0},{3,1},{4,6},{5,7},{6,4},{7,5},{8,10},{9,11},{10,... | collective-permute-start | bytes 301064 | tf_op jit(solution)/shard_map/ppermute | solution.py:211
  49.4 6.3 %collective-permute-start.16 = (bf16[8,6272]{1,0:T(8,128)(2,1)S(1)}, bf16[8,6272]{1,0:T(8,128)(2,1)S(1)}, u32[]{:S(2)}, u32[]{:S(2)}) collective-permute-start(bf16[8,6272]{1,0:T(8,128)(2,1)S(1)} %get-tuple-element.30.refs_0_), channel_id=1, source_target_pairs={{0,3},{1,2},{2,1},{3,0},{4,7},{5,6},{6,5},{7,4},{8,11},{9,10},{10,... | collective-permute-start | bytes 301064 | tf_op jit(solution)/shard_map/ppermute | solution.py:211
  57.3 4.4 %collective-permute-start.17 = (bf16[8,1792]{1,0:T(8,128)(2,1)S(1)}, bf16[8,1792]{1,0:T(8,128)(2,1)S(1)}, u32[]{:S(2)}, u32[]{:S(2)}) collective-permute-start(bf16[8,1792]{1,0:T(8,128)(2,1)S(1)} %shard_map.133.refs_0_), channel_id=1, source_target_pairs={{0,4},{4,0},{8,12},{12,8},{1,5},{5,1},{9,13},{13,9},{2,6},{6,2},{1... | collective-permute-start | bytes 86024 | tf_op jit(solution)/shard_map/ppermute | solution.py:211
  57.3 5.0 %collective-permute-start.18 = (bf16[8,1792]{1,0:T(8,128)(2,1)S(1)}, bf16[8,1792]{1,0:T(8,128)(2,1)S(1)}, u32[]{:S(2)}, u32[]{:S(2)}) collective-permute-start(bf16[8,1792]{1,0:T(8,128)(2,1)S(1)} %shard_map.133.refs_0_), channel_id=1, source_target_pairs={{0,8},{4,12},{8,0},{12,4},{1,9},{5,13},{9,1},{13,5},{2,10},{6,14},... | collective-permute-start | bytes 86024 | tf_op jit(solution)/shard_map/ppermute | solution.py:211
  59.6 5.7 %collective-permute-start.19 = (bf16[8,1792]{1,0:T(8,128)(2,1)S(1)}, bf16[8,1792]{1,0:T(8,128)(2,1)S(1)}, u32[]{:S(2)}, u32[]{:S(2)}) collective-permute-start(bf16[8,1792]{1,0:T(8,128)(2,1)S(1)} %shard_map.133.refs_0_), channel_id=1, source_target_pairs={{0,12},{4,8},{8,4},{12,0},{1,13},{5,9},{9,5},{13,1},{2,14},{6,10},... | collective-permute-start | bytes 86024 | tf_op jit(solution)/shard_map/ppermute | solution.py:211
